TPU v7x, 256 devices: a whole 4x4x8 slice. The times are simulated.
256 devices in a mesh: dp: 2 (over core), ctx: 32 (over z, y), head: 4 (over x).
Axes of the slice: x: 4, y: 4, z: 8, core: 2. Of those that a mesh axis runs over, the one named last changes fastest.
Arguments:
- x_raw: bfloat16 [2, 8192, 8192], P('dp', 'ctx', 'head'), may hold values from -6 to 6
- bc_raw: bfloat16 [2, 8192, 2, 1024], P('dp', 'ctx', None, 'head'), may hold values from -6 to 6
- z_gate: bfloat16 [2, 8192, 8192], P('dp', 'ctx', 'head'), may hold values from -20 to 20
- dt_raw: bfloat16 [2, 128, 8192], P('dp', 'head', 'ctx'), may hold values from -4 to 4
- resets: int32 [2, 8192], P('dp', 'ctx'), may hold values 0 or 1
- conv_x_weight: float32 [4, 8192], P(None, 'head'), may hold values from -3 to 3
- conv_x_bias: float32 [8192], P('head'), may hold values from -1.5 to 1.5
- conv_bc_weight: float32 [4, 2, 1024], P(None, None, 'head'), may hold values from -3 to 3
- conv_bc_bias: float32 [2, 1024], P(None, 'head'), may hold values from -1.5 to 1.5
- a_log: float32 [128], P('head'), may hold values from -9 to 1
- dt_bias: float32 [128], P('head'), may hold values from -13 to -3
- skip_weight: float32 [128], P('head'), may hold values from 0.5 to 2
- norm_gain: float32 [8192], P('head'), may hold values from 0.1 to 1.9
- grad_out: bfloat16 [2, 8192, 8192], P('dp', 'ctx', 'head'), may hold values from -6 to 6
Outputs:
- grad_x: bfloat16 [2, 8192, 8192], P('dp', 'ctx', 'head')
- grad_bc: bfloat16 [2, 8192, 2, 1024], P('dp', 'ctx', None, 'head')
- grad_z: bfloat16 [2, 8192, 8192], P('dp', 'ctx', 'head')
- grad_dt: float32 [2, 128, 8192], P('dp', 'head', 'ctx')
- grad_conv_x_weight: float32 [4, 8192], P(None, 'head')
- grad_conv_x_bias: float32 [8192], P('head')
- grad_conv_bc_weight: float32 [4, 2, 1024], P(None, None, 'head')
- grad_conv_bc_bias: float32 [2, 1024], P(None, 'head')
- grad_a_log: float32 [128], P('head')
- grad_dt_bias: float32 [128], P('head')
- grad_skip: float32 [128], P('head')
- grad_gain: float32 [8192], P('head')
All inputs are finite; a program needn't handle non-finite values. No bound on the sum of `resets` on one device may be relied on, other than what follows from the above.
Results may differ from a plain program's by a relative error of at most 0.01595.
Values may be sent and summed in bfloat16 or wider, within the bound.
A program may use at most 256 MiB of HBM per device.

v0:
```python
import functools

import jax
import jax.numpy as jnp
from jax import lax
from jax.sharding import PartitionSpec as P

HEAD_DIM = 64
NSTATE = 128
CONV = 4
STRETCH = 128
INNER = 8192


norm_eps = 1e-05


def from_behind(value, axis, steps):
    count = lax.axis_size(axis)
    first, last = (max(0, -steps), min(count, count - steps))
    return lax.ppermute(value, axis, [(source, source + steps) for source in range(first, last)])


def entering(value, axis, join, neutral, backward):
    count, mine = (lax.axis_size(axis), lax.axis_index(axis))
    pieces = jax.tree.map(lambda part: lax.all_gather(part, axis), value)
    if backward:
        pieces = jax.tree.map(lambda part: part[::-1], pieces)
        mine = count - 1 - mine
    running = jax.tree.map(
        lambda part, zero: jnp.full_like(part, 0) + jnp.asarray(zero, part.dtype), value, neutral
    )

    def step(position, running):
        longer = join(running, jax.tree.map(lambda part: part[position], pieces))
        return jax.tree.map(lambda new, old: jnp.where(position < mine, new, old), longer, running)

    return lax.fori_loop(0, count - 1, step, running)


def kept(value):
    return lax.optimization_barrier(value)


def causal_conv(extended, counts, weight, conv_bias):
    pad_rows = CONV - 1
    row_count = extended.shape[0] - pad_rows
    shape_tail = (1,) * (extended.ndim - 1)
    summed = conv_bias + weight[0] * extended[pad_rows:]
    for lag_step in range(1, CONV):
        lower = pad_rows - lag_step
        live_mask = (counts[pad_rows:] == counts[lower : lower + row_count]).astype(jnp.float32)
        summed = summed + weight[lag_step] * extended[
            lower : lower + row_count
        ] * live_mask.reshape((row_count,) + shape_tail)
    return kept(jax.nn.silu(summed).astype(jnp.bfloat16))


def rows_to_blocks(array_rows):
    return array_rows.reshape((array_rows.shape[0] // STRETCH, STRETCH) + array_rows.shape[1:])


def steps_to_blocks(steps_dt):
    shape_now = steps_dt.shape
    reshaped = steps_dt.reshape(shape_now[0], shape_now[1], shape_now[2] // STRETCH, STRETCH)
    return jnp.transpose(reshaped, (2, 0, 1, 3))


def from_before(block_c, prior_state, running, resets_seen):
    from_start = jnp.where(resets_seen == 0.0, jnp.exp(running), 0.0)
    state_half = prior_state.astype(jnp.bfloat16)
    carried = jnp.einsum("tgn,ghpn->tghp", block_c, state_half, preferred_element_type=jnp.float32)
    return carried * jnp.transpose(from_start, (2, 0, 1))[..., None]


def keep_factor(running, resets_seen):
    return jnp.where(resets_seen[-1] == 0.0, jnp.exp(running[..., -1]), 0.0)


def block_end(block_x, block_b, block_dt, running, resets_seen):
    to_end = jnp.where(resets_seen == resets_seen[-1], jnp.exp(running[..., -1:] - running), 0.0)
    scaled = (
        block_x.astype(jnp.float32) * jnp.transpose(block_dt * to_end, (2, 0, 1))[..., None]
    ).astype(jnp.bfloat16)
    return jnp.einsum("sghp,sgn->ghpn", scaled, block_b, preferred_element_type=jnp.float32)


def block_terms(prior_state, block_piece, decay_rate):
    block_x, block_b, block_c, block_dt, block_flags = block_piece
    running = jnp.cumsum(-decay_rate[:, :, None] * block_dt, axis=-1)
    resets_seen = jnp.cumsum(block_flags)
    position = jnp.arange(block_flags.shape[0])
    same_doc = (resets_seen[:, None] == resets_seen[None, :]) & (
        position[:, None] >= position[None, :]
    )
    spread = running[..., :, None] - running[..., None, :]
    segment = jnp.where(same_doc, jnp.exp(jnp.where(same_doc, spread, 0.0)), 0.0)
    scores = jnp.einsum("tgn,sgn->gts", block_c, block_b, preferred_element_type=jnp.float32)
    weights = (scores[:, None] * segment * block_dt[:, :, None, :]).astype(jnp.bfloat16)
    within = jnp.einsum("ghts,sghp->tghp", weights, block_x, preferred_element_type=jnp.float32)
    carried = from_before(block_c, prior_state, running, resets_seen)
    fresh_state = block_end(block_x, block_b, block_dt, running, resets_seen)
    next_state = keep_factor(running, resets_seen)[..., None, None] * prior_state + fresh_state
    return (next_state, within + carried)


def scan_blocks(inputs, b_rows, c_rows, steps_dt, decay_rate, reset_flags, state_in):
    row_count = inputs.shape[0]
    pieces = (
        rows_to_blocks(inputs),
        rows_to_blocks(b_rows),
        rows_to_blocks(c_rows),
        steps_to_blocks(steps_dt),
        rows_to_blocks(reset_flags),
    )
    stepper = functools.partial(block_terms, decay_rate=decay_rate)
    final_state, outputs = lax.scan(stepper, state_in, pieces)
    return (outputs.reshape((row_count,) + inputs.shape[1:]), final_state)


def block_ends(inputs, b_rows, steps_dt, decay_rate, reset_flags):

    def block_advance(carried_pair, block_piece):
        product, prior_state = carried_pair
        part_x, part_b, part_dt, part_flags = block_piece
        running = jnp.cumsum(-decay_rate[:, :, None] * part_dt, axis=-1)
        resets_seen = jnp.cumsum(part_flags)
        keep_all = keep_factor(running, resets_seen)
        fresh_state = block_end(part_x, part_b, part_dt, running, resets_seen)
        return ((product * keep_all, keep_all[..., None, None] * prior_state + fresh_state), None)

    start_pair = (
        jnp.ones(decay_rate.shape, jnp.float32),
        jnp.zeros(decay_rate.shape + (HEAD_DIM, NSTATE), jnp.float32),
    )
    pieces = (
        rows_to_blocks(inputs),
        rows_to_blocks(b_rows),
        steps_to_blocks(steps_dt),
        rows_to_blocks(reset_flags),
    )
    end_pair, unused = lax.scan(block_advance, start_pair, pieces)
    return end_pair


def carried_only(c_rows, steps_dt, decay_rate, reset_flags, prior_state):

    def carried_advance(state_now, block_piece):
        part_c, part_dt, part_flags = block_piece
        running = jnp.cumsum(-decay_rate[:, :, None] * part_dt, axis=-1)
        resets_seen = jnp.cumsum(part_flags)
        carried = from_before(part_c, state_now, running, resets_seen)
        return (keep_factor(running, resets_seen)[..., None, None] * state_now, carried)

    pieces = (rows_to_blocks(c_rows), steps_to_blocks(steps_dt), rows_to_blocks(reset_flags))
    final_state, outputs = lax.scan(carried_advance, prior_state, pieces)
    return outputs.reshape((c_rows.shape[0], c_rows.shape[1], steps_dt.shape[1], HEAD_DIM))


def gate_output(y_ssd, inputs, z_in, skip_weight):
    row_count = inputs.shape[0]
    skip_term = skip_weight.reshape(inputs.shape[1], inputs.shape[2])[
        None, :, :, None
    ] * inputs.astype(jnp.float32)
    mixed = kept((y_ssd + skip_term).astype(jnp.bfloat16))
    return mixed.astype(jnp.float32).reshape(row_count, -1) * jax.nn.silu(z_in)


def combine_pairs(earlier, later):
    return (earlier[0] * later[0], later[0][..., None, None] * earlier[1] + later[1])


def per_device(
    x_raw,
    bc_raw,
    z_gate,
    dt_raw,
    resets,
    conv_x_weight,
    conv_x_bias,
    conv_bc_weight,
    conv_bc_bias,
    a_log,
    dt_bias,
    skip_weight,
    norm_gain,
    grad_out,
):
    halo_rows = CONV - 1
    row_count = x_raw.shape[1]
    g_count = bc_raw.shape[3] // NSTATE
    heads_dev = a_log.shape[0]
    per_group = heads_dev // g_count
    reset_flags = resets[0].astype(jnp.float32)
    counts = jnp.cumsum(reset_flags)
    tail_keep = (counts[-halo_rows:] == counts[-1]).astype(jnp.float32)
    tail_half = tail_keep.astype(jnp.bfloat16)
    x_own = x_raw[0]
    bc_own = bc_raw[0]
    x_prev, bc_prev = from_behind(
        (x_own[-halo_rows:] * tail_half[:, None], bc_own[-halo_rows:] * tail_half[:, None, None]),
        "ctx",
        1,
    )
    x_ext = jnp.concatenate([x_prev, x_own]).astype(jnp.float32)
    bc_ext = jnp.concatenate([bc_prev, bc_own]).astype(jnp.float32)
    padded_counts = jnp.concatenate([jnp.zeros((halo_rows,), jnp.float32), counts])
    z_in = z_gate[0].astype(jnp.float32)
    dt_in = dt_raw[0].astype(jnp.float32)

    def conv_part(x_wide, bc_wide, dt_values, cx_weight, cx_bias, cb_weight, cb_bias, bias_dt):
        inputs = causal_conv(x_wide, padded_counts, cx_weight, cx_bias).reshape(
            row_count, g_count, per_group, HEAD_DIM
        )
        bc_conv = causal_conv(bc_wide, padded_counts, cb_weight, cb_bias)
        b_rows = bc_conv[:, 0].reshape(row_count, g_count, NSTATE)
        c_rows = bc_conv[:, 1].reshape(row_count, g_count, NSTATE)
        steps_dt = jax.nn.softplus(dt_values + bias_dt[:, None]).reshape(
            g_count, per_group, row_count
        )
        return (inputs, b_rows, c_rows, steps_dt)

    conv_outs, conv_pull = jax.vjp(
        conv_part,
        x_ext,
        bc_ext,
        dt_in,
        conv_x_weight,
        conv_x_bias,
        conv_bc_weight,
        conv_bc_bias,
        dt_bias,
    )
    inputs, b_rows, c_rows, steps_dt = conv_outs
    decay_rate = jnp.exp(a_log).reshape(g_count, per_group)
    device_decay, device_state = block_ends(inputs, b_rows, steps_dt, decay_rate, reset_flags)
    unit_decay = jnp.ones_like(device_decay)
    prefix_pair = entering(
        (device_decay, device_state),
        "ctx",
        combine_pairs,
        (unit_decay, jnp.zeros_like(device_state)),
        False,
    )
    state_in = prefix_pair[1]

    def ssd_part(block_inputs, block_b, block_c, block_dt, log_rate, prior_state):
        rate_now = jnp.exp(log_rate).reshape(g_count, per_group)
        return scan_blocks(
            block_inputs, block_b, block_c, block_dt, rate_now, reset_flags, prior_state
        )

    ssd_outs, ssd_pull = jax.vjp(ssd_part, inputs, b_rows, c_rows, steps_dt, a_log, state_in)
    y_ssd = ssd_outs[0]
    gated, post_pull = jax.vjp(gate_output, y_ssd, inputs, z_in, skip_weight)
    cotangent = grad_out[0].astype(jnp.float32)
    gained_out = cotangent * norm_gain
    row_totals = lax.psum(
        (jnp.sum(gated * gated, axis=-1), jnp.sum(gated * gained_out, axis=-1)), "head"
    )
    inv_rms = lax.rsqrt(row_totals[0] / INNER + norm_eps)
    d_gated = (
        gained_out * inv_rms[:, None]
        - gated * (inv_rms * inv_rms * inv_rms * row_totals[1] / INNER)[:, None]
    )
    gain_local = jnp.sum(cotangent * gated * inv_rms[:, None], axis=0)
    dy_ssd, d_inputs_post, d_z, d_skip = post_pull(d_gated)
    carried_map = functools.partial(carried_only, c_rows, steps_dt, decay_rate, reset_flags)
    unused_out, carried_pull = jax.vjp(carried_map, state_in)
    direct_adjoint = carried_pull(dy_ssd)[0]
    later_pair = entering(
        (device_decay, direct_adjoint),
        "ctx",
        combine_pairs,
        (unit_decay, jnp.zeros_like(direct_adjoint)),
        True,
    )
    d_inputs, d_b, d_c, d_dt, d_alog, d_state = ssd_pull((dy_ssd, later_pair[1]))
    d_inputs = d_inputs + d_inputs_post
    d_x_ext, d_bc_ext, d_dt_in, d_cxw, d_cxb, d_cbw, d_cbb, d_dt_bias = conv_pull(
        (d_inputs, d_b, d_c, d_dt)
    )
    back_x, back_bc = from_behind((d_x_ext[:halo_rows], d_bc_ext[:halo_rows]), "ctx", -1)
    grad_x_rows = jnp.concatenate(
        [d_x_ext[halo_rows:row_count], d_x_ext[row_count:] + back_x * tail_keep[:, None]]
    )
    grad_bc_rows = jnp.concatenate(
        [d_bc_ext[halo_rows:row_count], d_bc_ext[row_count:] + back_bc * tail_keep[:, None, None]]
    )
    local_terms = (d_cxw, d_cxb, d_cbw, d_cbb, d_alog, d_dt_bias, d_skip, gain_local)
    summed_terms = lax.psum(
        (
            local_terms[0],
            local_terms[1],
            local_terms[2],
            local_terms[3],
            local_terms[4],
            local_terms[5],
            local_terms[6],
            local_terms[7],
        ),
        ("dp", "ctx"),
    )
    grad_scale = float(lax.axis_size("dp") * lax.axis_size("ctx") * row_count) ** (-0.5)
    return (
        grad_x_rows[None].astype(jnp.bfloat16),
        grad_bc_rows[None].astype(jnp.bfloat16),
        d_z[None].astype(jnp.bfloat16),
        d_dt_in[None],
        summed_terms[0] * grad_scale,
        summed_terms[1] * grad_scale,
        summed_terms[2] * grad_scale,
        summed_terms[3] * grad_scale,
        summed_terms[4] * grad_scale,
        summed_terms[5] * grad_scale,
        summed_terms[6] * grad_scale,
        summed_terms[7] * grad_scale,
    )


def solution(mesh):
    return jax.shard_map(
        per_device,
        mesh=mesh,
        in_specs=(
            P("dp", "ctx", "head"),
            P("dp", "ctx", None, "head"),
            P("dp", "ctx", "head"),
            P("dp", "head", "ctx"),
            P("dp", "ctx"),
            P(None, "head"),
            P("head"),
            P(None, None, "head"),
            P(None, "head"),
            P("head"),
            P("head"),
            P("head"),
            P("head"),
            P("dp", "ctx", "head"),
        ),
        out_specs=(
            P("dp", "ctx", "head"),
            P("dp", "ctx", None, "head"),
            P("dp", "ctx", "head"),
            P("dp", "head", "ctx"),
            P(None, "head"),
            P("head"),
            P(None, None, "head"),
            P(None, "head"),
            P("head"),
            P("head"),
            P("head"),
            P("head"),
        ),
        check_vma=False,
    )
```

profile of v0, /device:TPU:128, one launch (start us, length us, event | category | flops | bytes accessed | tf_op | source)
XLA Modules:
  0.0 1191.2 jit_solution(14840181272702812922)
XLA Ops:
  17.0 3.5 collective-permute-start.1
  30.2 3.7 multiply_convert_fusion.7
  41.4 11.3 while.160
  61.7 10.0 while.158
  74.3 41.9 %all-gather.3 = f32[32,2,16]{2,1,0:T(2,128)S(1)} all-gather(f32[1,2,16]{2,1,0:T(2,128)S(1)} %bitcast.631), channel_id=2, replica_groups=mesh['dp'=2,'ctx'=32,'head'=4] {'ctx'}, dimensions={0}, use_global_device_ids=true | all-gather | bytes 4224 | tf_op jit(solution)/shard_map/all_gather | solution.py:26
  116.3 168.9 %all-gather.7.cloned.1.call-done = f32[64,16,64,128]{3,2,1,0:T(8,128)} async-done(((f32[2,16,64,128]{3,2,1,0:T(8,128)}), f32[64,16,64,128]{3,2,1,0:T(8,128)}) %all-gather.7.cloned.1.call-update) | async-done | bytes 33554448 | tf_op jit(solution)/shard_map/all_gather | solution.py:26
  285.2 46.6 %while.161 = (s32[]{:T(128)}, f32[2,16,64,128]{3,2,1,0:T(8,128)S(1)}, s32[]{:T(128)}, f32[32,2,16]{2,1,0:T(2,128)S(1)}, f32[32,2,16,64,128]{4,3,2,1,0:T(8,128)}, /*index=5*/s32[]{:T(128)}, s32[]{:T(128)}) while((s32[]{:T(128)}, f32[2,16,64,128]{3,2,1,0:T(8,128)S(1)}, s32[]{:T(128)}, f32[32,2,16]{2,1,0:T(2,128)S(1)}, ...), condition=%wide.region_7.8_spmd.clone, body=%wide.region_6.7_spmd.clone.sunk | while | flops 1048580 | bytes 3146225 | solution.py:38
  334.8 110.5 %while.159 = (s32[]{:T(128)}, f32[2,16,64,128]{3,2,1,0:T(8,128)S(1)}, f32[2,128,2,16,64]{1,0,4,3,2:T(2,128)}, pred[2,2,16,128,128]{4,3,2,1,0:T(32,128)(4,1)}, f3...) while((s32[]{:T(128)}, ...), condition=%wide.region_11.12_spmd.clone, body=%wide.region_8.11_spmd.clone.sunk | while | flops 222142656 | bytes 67194320 | solution.py:117
  350.2 25.0 %dynamic_update_slice.324 = f32[2,128,2,16,64]{1,0,4,3,2:T(2,128)} dynamic-update-slice(f32[2,128,2,16,64]{1,0,4,3,2:T(2,128)} %get-tuple-element.3483, f32[1,128,2,16,64]{1,0,4,3,2:T(1,128)} %bitcast.609, s32[]{:T(128)S(6)} %copy.383, s32[]{:T(128)} %constant.352.clone.1..sunk, s32[]{:T(128)} %constant.352.clone.1..sunk, s32[]{:T(128)} %constant.352.clone.1..sunk, s32[]{:T(128)} %constant.352.clone.1..sunk) | dynamic-update-slice | bytes 2097156 | tf_op jit(solution)/shard_map/jvp()/while/body/jit(dynamic_update_index_in_dim)/dynamic_update_slice | solution.py:117
  376.9 4.0 fusion.249
  405.4 25.0 %dynamic_update_slice.324 = f32[2,128,2,16,64]{1,0,4,3,2:T(2,128)} dynamic-update-slice(f32[2,128,2,16,64]{1,0,4,3,2:T(2,128)} %get-tuple-element.3483, f32[1,128,2,16,64]{1,0,4,3,2:T(1,128)} %bitcast.609, s32[]{:T(128)S(6)} %copy.383, s32[]{:T(128)} %constant.352.clone.1..sunk, s32[]{:T(128)} %constant.352.clone.1..sunk, s32[]{:T(128)} %constant.352.clone.1..sunk, s32[]{:T(128)} %constant.352.clone.1..sunk) | dynamic-update-slice | bytes 2097156 | tf_op jit(solution)/shard_map/jvp()/while/body/jit(dynamic_update_index_in_dim)/dynamic_update_slice | solution.py:117
  432.2 4.0 fusion.249
  445.3 4.3 reshape.606
  454.0 10.4 all-reduce.22
  482.6 4.1 fusion.159
  489.2 210.1 %all-gather.9.cloned.1.call-done = f32[64,16,64,128]{3,2,1,0:T(8,128)} async-done(((f32[2,16,64,128]{3,2,1,0:T(8,128)}), f32[64,16,64,128]{3,2,1,0:T(8,128)}) %all-gather.9.cloned.1.call-update) | async-done | bytes 33554448 | tf_op jit(solution)/shard_map/all_gather | solution.py:26
  699.3 23.3 %rev.7 = f32[32,2,16,64,128]{4,3,2,1,0:T(8,128)} reverse(f32[32,2,16,64,128]{4,3,2,1,0:T(8,128)} %bitcast.608), dimensions={0} | reverse | bytes 67108864 | tf_op jit(solution)/shard_map/rev | solution.py:28
  722.6 46.6 %while.163 = (s32[]{:T(128)}, f32[2,16,64,128]{3,2,1,0:T(8,128)S(1)}, s32[]{:T(128)}, f32[32,2,16]{2,1,0:T(2,128)S(1)}, f32[32,2,16,64,128]{4,3,2,1,0:T(8,128)}, /*index=5*/s32[]{:T(128)}, s32[]{:T(128)}) while((s32[]{:T(128)}, f32[2,16,64,128]{3,2,1,0:T(8,128)S(1)}, s32[]{:T(128)}, f32[32,2,16]{2,1,0:T(2,128)S(1)}, ...), condition=%wide.region_23.24_spmd.clone, body=%wide.region_22.23_spmd.clone.sunk | while | flops 1048580 | bytes 3146225 | solution.py:38
  772.7 91.6 %while.164 = (s32[]{:T(128)}, f32[2,16]{1,0:T(2,128)}, f32[2,16,64,128]{3,2,1,0:T(8,128)S(1)}, bf16[2,128,2,16,64]{1,4,3,2,0:T(8,128)(2,1)}, bf16[2,128,2,128]{3...) while((s32[]{:T(128)}, f32[2,16]{1,0:T(2,128)}, ...), condition=%wide.region_35.36_spmd.clone, body=%wide.region_24.35_spmd.clone.sunk | while | flops 431345728 | bytes 55708368 | solution.py:117
  780.7 5.2 fusion.275
  826.5 5.2 fusion.275
  867.9 4.3 multiply_reduce_fusion.3
  881.2 5.1 collective-permute-start.2
  899.3 274.8 %all-reduce.21 = (f32[4,2048]{1,0:T(4,128)S(1)}, f32[2048]{0:T(1024)}, f32[4,2,256]{2,1,0:T(2,128)S(1)}, f32[2,256]{1,0:T(2,128)}, f32[32]{0:T(128)}, /*index=5*/f32[32]{0:T(128)}, f32[32]{0:T(128)}, f32[2048]{0:T(1024)}) all-reduce(f32[4,2048]{1,0:T(4,128)S(1)} %pad_add_fusion.4, ...), channel_id=1, replica_groups=mesh['dp'=2,'ctx'=32,'head'=4] {'dp','ctx'}, use_global_device_ids=true, to_apply=%region_40.41 | all-reduce | flops 14944 | bytes 119552 | tf_op jit(solution)/shard_map/psum | solution.py:291
  (780 shorter events, 347.1 us)
Async XLA Ops:
  7.2 21.0 %copy-start.120 = (f32[2,256]{1,0:T(2,128)S(1)}, f32[2,256]{1,0:T(2,128)}, u32[]{:S(2)}) copy-start(f32[2,256]{1,0:T(2,128)} %param.36) | copy-start | bytes 6148
  7.2 278.0 %all-gather.7.cloned.1.call-start = ((), (), s32[]{:S(2)}) async-start(), calls=%async_computation | async-start | bytes 34603008 | tf_op jit(solution)/shard_map/all_gather | solution.py:26
  12.5 17.1 %collective-permute-start = (bf16[3,2048]{1,0:T(4,128)(2,1)S(1)}, bf16[3,2048]{1,0:T(4,128)(2,1)S(1)}, u32[]{:S(2)}, u32[]{:S(2)}) collective-permute-start(bf16[3,2048]{1,0:T(4,128)(2,1)S(1)} %bitcast_multiply_fusion.16), channel_id=1, source_target_pairs={{0,4},{4,8},{8,12},{12,16},{16,20},{20,24},{24,28},{28,32},{32,36}... | collective-permute-start | bytes 36872 | tf_op jit(solution)/shard_map/ppermute | solution.py:21
  17.0 10.2 collective-permute-start.1
  20.6 8.8 copy-start.86
  20.6 8.8 copy-start.90
  20.6 8.8 copy-start.94
  53.7 645.6 %all-gather.9.cloned.1.call-start = ((), (), s32[]{:S(2)}) async-start(), calls=%async_computation.1 | async-start | bytes 34603008 | tf_op jit(solution)/shard_map/all_gather | solution.py:26
  376.9 7.3 copy-start.73
  376.9 7.9 copy-start.64
  376.9 7.9 copy-start.66
  432.2 7.3 copy-start.73
  432.2 7.9 copy-start.64
  432.2 7.9 copy-start.66
  453.1 11.4 copy-start.14
  880.8 10.7 copy-start.49
  880.8 10.7 copy-start.50
  880.8 10.7 copy-start.118
  881.2 12.0 %copy-start.85 = (bf16[1,32,256]{2,1,0:T(8,128)(2,1)S(1)}, bf16[1,32,256]{2,1,0:T(8,128)(2,1)}, u32[]{:S(2)}) copy-start(bf16[1,32,256]{2,1,0:T(8,128)(2,1)} %param.31) | copy-start | bytes 49156
  881.2 300.9 %collective-permute-start.2 = (f32[3,2048]{1,0:T(4,128)S(1)}, f32[3,2048]{1,0:T(4,128)S(1)}, u32[]{:S(2)}, u32[]{:S(2)}) collective-permute-start(f32[3,2048]{1,0:T(4,128)S(1)} %copy-done.101), channel_id=1, source_target_pairs={{4,0},{8,4},{12,8},{16,12},{20,16},{24,20},{28,24},{32,28},{36,32}... | collective-permute-start | bytes 73736 | tf_op jit(solution)/shard_map/ppermute | solution.py:21
  887.6 292.6 %collective-permute-start.3 = (f32[3,2,256]{2,0,1:T(4,128)}, f32[3,2,256]{2,0,1:T(4,128)}, u32[]{:S(2)}, u32[]{:S(2)}) collective-permute-start(f32[3,2,256]{2,0,1:T(4,128)} %pad_add_fusion.5), channel_id=1, source_target_pairs={{4,0},{8,4},{12,8},{16,12},{20,16},{24,20},{28,24},{32,28},{36,32}... | collective-permute-start | bytes 18440 | tf_op jit(solution)/shard_map/ppermute | solution.py:21
  893.2 287.9 %copy-start.55 = (bf16[1,253,2,256]{3,1,2,0:T(8,128)(2,1)S(1)}, bf16[1,253,2,256]{3,1,2,0:T(8,128)(2,1)}, u32[]{:S(2)}) copy-start(bf16[1,253,2,256]{3,1,2,0:T(8,128)(2,1)} %fusion.164) | copy-start | bytes 777220
  1174.0 8.0 copy-start.9
  1174.1 8.0 copy-start.116
  (153 other events, 466.7 us)
Sparse Core Ops, SparseCore 0:
  53.8 231.3 all-gather.6
  471.0 228.2 all-gather.8
where the time goes:
time: 1200 us; the launch traced here: 1190 us
  waiting for transfers between devices  379 us (32%)
  blocking collectives  327 us (27%)
  other arithmetic  217 us (18%)
  local copies, waits for them, and re-layouts  198 us (16%)
  matrix products  32.7 us (3%)
  starting transfers between devices  15.2 us (1%)
  between operations  15 us (1%)
    all_gather x2, waiting for transfers between devices, entering(): pieces = jax.tree.map(lambda part: lax.all_gather(part, axis), value)  379 us
    psum x1, blocking collectives, per_device(): lax.psum((local_terms[0], local_terms[1], local_terms[2], local_terms[3],...  275 us
    select_n x62, other arithmetic, step(): jnp.where(position < mine, new, old)  90.6 us
    dynamic_update_slice x20, local copies, waits for them, and re-layouts, scan_blocks(): final_state, outputs = lax.scan(stepper, state_in, pieces)  65.8 us
    all_gather x1, blocking collectives, entering(): pieces = jax.tree.map(lambda part: lax.all_gather(part, axis), value)  41.9 us
  transfers between devices with their start and end apart: 6, of which 2 were waited for; matrix products, arithmetic and copies ran while one was open for 5% of the time, Pallas kernels for 0%

commit v1 on v0

v1 whole, which is shorter than its diff:
```python
import functools

import jax
import jax.numpy as jnp
from jax import lax
from jax.experimental import pallas as pl
from jax.experimental.pallas import tpu as pltpu
from jax.sharding import PartitionSpec as P

F32 = jnp.float32
BF16 = jnp.bfloat16
HIGHEST = lax.Precision.HIGHEST
MESH = pl.DeviceIdType.MESH

HEAD_DIM = 64
NSTATE = 128
CONV = 4
INNER = 8192
EPS = 1e-05

T = 256
B = 128
H = 32
D = 2048
DB = 512
NT = D // 128
NG = 2
TPG = NT // NG
ROWS = 16
VM = pl.BlockSpec(memory_space=pltpu.VMEM)
SM = pl.BlockSpec(memory_space=pltpu.SMEM)
VLIM = 60 * 1024 * 1024


def dnn(a, b):
    return lax.dot_general(a, b, (((1,), (0,)), ((), ())), preferred_element_type=F32)


def dnt(a, b):
    return lax.dot_general(a, b, (((1,), (1,)), ((), ())), preferred_element_type=F32)


def dtn(a, b):
    return lax.dot_general(a, b, (((0,), (0,)), ((), ())), preferred_element_type=F32)


def dnn_full(a, b):
    return lax.dot_general(
        a, b, (((1,), (0,)), ((), ())), precision=HIGHEST, preferred_element_type=F32
    )


def dnt_full(a, b):
    return lax.dot_general(
        a, b, (((1,), (1,)), ((), ())), precision=HIGHEST, preferred_element_type=F32
    )


def iota(shape, dim):
    return lax.broadcasted_iota(jnp.int32, shape, dim)


def high_low(v):
    high = v.astype(BF16).astype(F32)
    return high, v - high


def sigmoid(v):
    return 1.0 / (1.0 + jnp.exp(-v))


def softplus(v):
    y = jnp.exp(-jnp.abs(v))
    series = y * (1.0 - y * (0.5 - y * (1.0 / 3.0 - y * (0.25 - 0.2 * y))))
    return jnp.maximum(v, 0.0) + jnp.where(y < 0.02, series, jnp.log(1.0 + y))


def lanes(j):
    return pl.ds(pl.multiple_of(j * 128, 128), 128)


def spread_two(j):
    row = iota((2 * H, 128), 0) % H
    lane = iota((2 * H, 128), 1)
    return (row == 2 * j + lane // HEAD_DIM).astype(BF16)


def spread_pair(j):
    row = iota((128, 256), 0)
    lane = iota((128, 256), 1)
    return ((row % H == 2 * j + lane // 128) & (row < 3 * H)).astype(BF16)


def collect_two(j):
    row = iota((H, 128), 0)
    lane = iota((H, 128), 1)
    return (row == 2 * j + lane // HEAD_DIM).astype(BF16)


def head_sums(j, v):
    high = v.astype(BF16)
    low = (v - high.astype(F32)).astype(BF16)
    e = collect_two(j)
    return dnt(e, high) + dnt(e, low)


def shift_extend(ext, main, halo):
    ext[0:8, :] = halo
    ext[8 : 8 + T, :] = main


def conv_input(ext, live, w, bias):
    u = bias + w[0] * ext[8 : 8 + T, :]
    for k in range(1, CONV):
        u = u + w[k] * ext[8 - k : 8 - k + T, :] * live[k - 1]
    return u


def live_masks(cnt, live):
    now = cnt[8 : 8 + T, :]
    for k in range(1, CONV):
        live[k - 1] = (now == cnt[8 - k : 8 - k + T, :]).astype(F32)


def block_mask(rt, q, c):
    qc = rt[c * B : (c + 1) * B, H : H + 1]
    qr = q[0:1, c * B : (c + 1) * B]
    ok = (qc == qr) & (iota((B, B), 0) >= iota((B, B), 1))
    return jnp.where(ok, 0.0, -1e30)


def row_state(ref, j, n, lead):
    ncq = n // 8
    tpc = NT // ncq
    cq = j // tpc
    lane = lanes(j % tpc)
    return jnp.concatenate([ref[rz * ncq + cq, :, lane] for rz in range(8)], axis=0)


def put_state(ref, j, n, v):
    ncq = n // 8
    tpc = NT // ncq
    cq = j // tpc
    lane = lanes(j % tpc)
    for rz in range(8):
        ref[rz * ncq + cq, :, lane] = v[rz * ROWS : (rz + 1) * ROWS]


def k1_body(
    n, x, bc, halo, dtr, flg, hp, cxw, cxb, cbw, cbb,
    xc_o, bcc_o, dt_o, r_o, mt_o, rt_o, rs_o, q_o, st_o, kr_o, fr_o,
    ext, cnt, live,
):
    rate = jnp.exp(hp[:, 0:1])
    bias = hp[:, 1:2]
    tri = (iota((B, B), 0) <= iota((B, B), 1)).astype(F32)
    before = jnp.zeros((8, 1), F32)
    cnt[0:8, :] = jnp.zeros((8, 128), F32)
    for c in range(2):
        sl = slice(c * B, (c + 1) * B)
        dtv = softplus(dtr[:, sl].astype(F32) + bias)
        r = dnn_full(-rate * dtv, tri)
        q = dnn(jnp.broadcast_to(flg[:, sl].astype(F32), (8, B)), tri)
        rl = r[:, B - 1 : B]
        ql = q[:, B - 1 : B]
        dtte = dtv * jnp.where(q[0:1] == ql[0:1], jnp.exp(rl - r), 0.0)
        fs = jnp.where(q[0:1] == 0.0, jnp.exp(r), 0.0)
        dt_o[c] = dtv
        r_o[c] = r
        q_o[:, sl] = q
        a1, a2 = high_low(dtte)
        b1, b2 = high_low(fs)
        mt_o[sl, :] = jnp.concatenate([a1, a2, b1, b2], axis=0).T.astype(BF16)
        dev = q + before
        before = dev[:, B - 1 : B]
        rt = jnp.concatenate([r, q, dev, jnp.zeros((80, B), F32)], axis=0).T
        rt_o[sl, :] = rt
        r1, r2 = high_low(r)
        r2, r3 = high_low(r2)
        rs_o[sl, :] = jnp.concatenate([r1, r2, r3, jnp.zeros((H, B), F32)], axis=0).T.astype(BF16)
        cnt[8 + c * B : 8 + (c + 1) * B, :] = jnp.broadcast_to(rt[:, H + 8 : H + 9], (B, 128))
    live_masks(cnt, live)

    for j in range(4):
        sl = slice(j * 128, (j + 1) * 128)
        shift_extend(ext, bc[:, sl].astype(F32), halo[:, D + j * 128 : D + (j + 1) * 128].astype(F32))
        u = conv_input(ext, live, [cbw[k : k + 1, sl] for k in range(CONV)], cbb[0:1, sl])
        bcc_o[:, sl] = (u * sigmoid(u)).astype(BF16)

    for g in range(NG):
        bt = [
            bcc_o[c * B : (c + 1) * B, g * 128 : (g + 1) * 128].astype(F32).T.astype(BF16)
            for c in range(2)
        ]

        def tile(jj, carry, g=g, bt=bt):
            j = g * TPG + jj
            sl = lanes(j)
            shift_extend(ext, x[:, sl].astype(F32), halo[:, sl].astype(F32))
            u = conv_input(ext, live, [cxw[k : k + 1, sl] for k in range(CONV)], cxb[0:1, sl])
            xc = (u * sigmoid(u)).astype(BF16)
            xc_o[:, sl] = xc
            e2 = spread_two(j)
            dtte = dnn(mt_o[:, 0 : 2 * H], e2)
            uu = (xc.astype(F32) * dtte).astype(BF16)
            k0 = dnn(mt_o[B - 16 : B, 2 * H : 4 * H], e2)[15:16]
            k1 = dnn(mt_o[T - 16 : T, 2 * H : 4 * H], e2)[15:16]
            fresh0 = dnn(bt[0], uu[0:B])
            fresh1 = dnn(bt[1], uu[B:T])
            fr_o[:, sl] = fresh0
            put_state(st_o, j, n, (k1 * fresh0 + fresh1).astype(BF16))
            ncq = n // 8
            tpc = NT // ncq
            kr_o[j // tpc, :, lanes(j % tpc)] = k0 * k1
            return carry

        lax.fori_loop(0, TPG, tile, 0)


def scan_body(n, first, *refs):
    if first:
        st, kr, out, kall, rb, pb, ob, kb, s1, r1, s2, r2, sk, rk = refs
    else:
        st, kall, out, rb, pb, ob, s1, r1, s2, r2 = refs
    ncq = n // 8
    me = lax.axis_index("ctx")
    barrier = pltpu.get_barrier_semaphore()

    def greet(k, carry):
        pl.semaphore_signal(
            barrier, inc=1, device_id={"ctx": lax.rem(me + k, n)}, device_id_type=MESH
        )
        return carry

    lax.fori_loop(1, n, greet, 0)
    rb[me] = st[me]
    if first:
        kb[me] = kr[lax.rem(me, ncq)]
    pl.semaphore_wait(barrier, n - 1)

    def state_copy(src, dst_slot, dev, sem_s, sem_r):
        return pltpu.make_async_remote_copy(
            src_ref=src, dst_ref=dst_slot, send_sem=sem_s, recv_sem=sem_r,
            device_id={"ctx": dev}, device_id_type=MESH,
        )

    def send(k, carry):
        to = lax.rem(me + k, n)
        state_copy(st.at[to], rb.at[me], to, s1.at[to], r1.at[me]).start()
        if first:
            state_copy(kr.at[lax.rem(to, ncq)], kb.at[me], to, sk.at[to], rk.at[me]).start()
        return carry

    lax.fori_loop(1, n, send, 0)

    def step(i, acc):
        d = i if first else n - 1 - i

        @pl.when(d != me)
        def _():
            state_copy(st.at[d], rb.at[d], d, s1.at[d], r1.at[d]).wait_recv()
            if first:
                state_copy(kr.at[0], kb.at[d], d, sk.at[d], rk.at[d]).wait_recv()

        pb[d] = acc.astype(BF16)

        @pl.when(d != me)
        def _():
            state_copy(pb.at[d], ob.at[me], d, s2.at[d], r2.at[me]).start()

        decay = kb[d] if first else kall[d]
        return decay * acc + rb[d].astype(F32)

    lax.fori_loop(0, n, step, jnp.zeros(rb.shape[1:], F32))
    ob[me] = pb[me]

    def finish(k, carry):
        d = lax.rem(me + k, n)
        state_copy(st.at[d], rb.at[d], d, s1.at[d], r1.at[d]).wait_send()
        if first:
            state_copy(kr.at[0], kb.at[d], d, sk.at[d], rk.at[d]).wait_send()
        state_copy(pb.at[d], ob.at[d], d, s2.at[d], r2.at[d]).wait()
        return carry

    lax.fori_loop(1, n, finish, 0)
    out[...] = ob[...]
    if first:
        kall[...] = kb[...]


def k2_body(
    n, xc, bcc, dt, r, rt, rs, mt, q, sin, fr, z, g_in, gain, skip,
    y_o, mixed_o, sums_o, sb1_o, acc,
):
    acc[...] = jnp.zeros_like(acc)
    half = iota((B, 128), 1) < HEAD_DIM
    for g in range(NG):
        for c in range(2):
            sl = slice(c * B, (c + 1) * B)
            mask = block_mask(rt, q, c)
            bb = bcc[sl, g * 128 : (g + 1) * 128]
            cc = bcc[sl, 256 + g * 128 : 256 + (g + 1) * 128]
            gm = dnt(cc, bb)

            def tile(jj, carry, g=g, c=c, sl=sl, mask=mask, cc=cc, gm=gm):
                j = g * TPG + jj
                ln = lanes(j)
                e2 = spread_two(j)
                rb2 = dnn(rs[sl, :], spread_pair(j))
                ws = []
                for i in range(2):
                    h = 2 * j + i
                    lm = jnp.exp(rb2[:, i * B : (i + 1) * B] - r[c, pl.ds(h, 1), :] + mask)
                    ws.append((gm * lm * dt[c, pl.ds(h, 1), :]).astype(BF16))
                xt = xc[sl, ln]
                zero = jnp.zeros_like(xt)
                xbd = jnp.concatenate([jnp.where(half, xt, zero), jnp.where(half, zero, xt)], axis=0)
                within = dnn(jnp.concatenate(ws, axis=1), xbd)
                sb = row_state(sin, j, n, 0)
                if c == 1:
                    k0 = dnn(mt[B - 16 : B, 2 * H : 4 * H], e2)[15:16]
                    sb = (k0 * sb.astype(F32) + fr[:, ln]).astype(BF16)
                    sb1_o[:, ln] = sb
                fs = dnn(mt[sl, 2 * H : 4 * H], e2)
                y = within + dnn(cc, sb) * fs
                y_o[sl, ln] = y
                lane = iota((1, 128), 1)
                sk = jnp.where(lane < HEAD_DIM, skip[2 * j], skip[2 * j + 1])
                mixed = (y + sk * xt.astype(F32)).astype(BF16)
                mixed_o[sl, ln] = mixed
                zf = z[sl, ln].astype(F32)
                gated = mixed.astype(F32) * (zf * sigmoid(zf))
                gained = g_in[sl, ln].astype(F32) * gain[0:1, ln]
                acc[0, sl, :] += gated * gated
                acc[1, sl, :] += gated * gained
                return carry

            lax.fori_loop(0, TPG, tile, 0)
    ones = jnp.ones((8, 128), F32)
    sums_o[0:8, :] = dnt_full(ones, acc[0])
    sums_o[8:16, :] = dnt_full(ones, acc[1])


def norm_body(n, s_in, out, buf, ss, rr):
    me = lax.axis_index("head")
    barrier = pltpu.get_barrier_semaphore()
    for k in range(1, n):
        pl.semaphore_signal(
            barrier, inc=1, device_id={"head": lax.rem(me + k, n)}, device_id_type=MESH
        )
    pl.semaphore_wait(barrier, n - 1)
    copies = []
    for k in range(1, n):
        copies.append(
            pltpu.make_async_remote_copy(
                src_ref=s_in, dst_ref=buf.at[k], send_sem=ss.at[k], recv_sem=rr.at[k],
                device_id={"head": lax.rem(me + k, n)}, device_id_type=MESH,
            )
        )
        copies[-1].start()
    for cp in copies:
        cp.wait()
    parts = [s_in[...]] + [buf[k] for k in range(1, n)]
    total = jnp.zeros_like(parts[0])
    for d in range(n):
        for k in range(n):
            total = total + jnp.where(lax.rem(me - k + n, n) == d, parts[k], 0.0)
    out[...] = total


def k3_body(
    n, sums, mixed, z, g_in, gain, y, xc, mt, bcc,
    dz_o, dy_o, rho_o, drow_o, ad_o, dsb1_o, inv_s, coef_s,
):
    ss = sums[0:8, :]
    sg = sums[8:16, :]
    inv = lax.rsqrt(ss / INNER + EPS)
    coef = inv * inv * inv * sg / INNER
    for c in range(2):
        sl = slice(c * B, (c + 1) * B)
        tr = jnp.concatenate([inv[:, sl], coef[:, sl], jnp.zeros((112, B), F32)], axis=0).T
        inv_s[sl, :] = jnp.broadcast_to(tr[:, 0:1], (B, 128))
        coef_s[sl, :] = jnp.broadcast_to(tr[:, 8:9], (B, 128))
    rho_o[...] = jnp.zeros_like(rho_o)
    drow_o[...] = jnp.zeros_like(drow_o)
    for g in range(NG):
        ct = [
            bcc[c * B : (c + 1) * B, 256 + g * 128 : 256 + (g + 1) * 128].astype(F32).T.astype(BF16)
            for c in range(2)
        ]

        def tile(jj, carry, g=g, ct=ct):
            j = g * TPG + jj
            ln = lanes(j)
            e2 = spread_two(j)
            m = mixed[:, ln].astype(F32)
            zf = z[:, ln].astype(F32)
            go = g_in[:, ln].astype(F32)
            sig = sigmoid(zf)
            sl = zf * sig
            gated = m * sl
            iv = inv_s[...]
            dg = go * gain[0:1, ln] * iv - gated * coef_s[...]
            drow_o[0:1, ln] = jnp.sum(go * gated * iv, axis=0, keepdims=True)
            dz_o[:, ln] = (dg * m * (sig * (1.0 + zf * (1.0 - sig)))).astype(BF16)
            dm = (dg * sl).astype(BF16)
            dy_o[:, ln] = dm
            dy = dm.astype(F32)
            drow_o[1:2, ln] = jnp.sum(dy * xc[:, ln].astype(F32), axis=0, keepdims=True)
            rho_o[...] += head_sums(j, dy * y[:, ln])
            fs = dnn(mt[:, 2 * H : 4 * H], e2)
            fd = (fs * dy).astype(BF16)
            d0 = dnn(ct[0], fd[0:B]).astype(BF16)
            d1 = dnn(ct[1], fd[B:T]).astype(BF16)
            dsb1_o[:, ln] = d1
            put_state(ad_o, j, n, (fs[B - 1 : B] * d1.astype(F32) + d0.astype(F32)).astype(BF16))
            return carry

        lax.fori_loop(0, TPG, tile, 0)


def conv_backward(ext, vk, live, w, bias, dxc):
    u = conv_input(ext, live, w, bias)
    s = sigmoid(u)
    du = dxc.astype(BF16).astype(F32) * (s * (1.0 + u * (1.0 - s)))
    rows = [jnp.sum(du * ext[8 : 8 + T, :], axis=0, keepdims=True)]
    vk[0, 8 : 8 + T, :] = du
    for k in range(1, CONV):
        v = du * live[k - 1]
        rows.append(jnp.sum(v * ext[8 - k : 8 - k + T, :], axis=0, keepdims=True))
        vk[k, 8 : 8 + T, :] = v
    rows.append(jnp.sum(du, axis=0, keepdims=True))
    own = w[0] * du
    before = jnp.zeros((8, 128), F32)
    for k in range(1, CONV):
        own = own + w[k] * vk[k, 8 + k : 8 + k + T, :]
        before = before + w[k] * vk[k, k : k + 8, :]
    return own, before, rows


def k4_body(
    n, x, bc, halo, dtr, hp, cxw, cxb, cbw, cbb, xc, bcc, dt, r, rt, rs, mt, q, dy, rho, dsb1,
    sin, sb1, later, drow, skip,
    gx_o, gbc_o, gdt_o, tail_o, hb_o, pk_o, ph_o,
    ext, cnt, live, vk, acc, kap, tl, dbc,
):
    half = iota((B, 128), 1) < HEAD_DIM
    cnt[0:8, :] = jnp.zeros((8, 128), F32)
    cnt[8 : 8 + T, :] = jnp.broadcast_to(rt[:, H + 8 : H + 9], (T, 128))
    live_masks(cnt, live)
    vk[:, 0:8, :] = jnp.zeros((CONV, 8, 128), F32)
    vk[:, 8 + T :, :] = jnp.zeros((CONV, 8, 128), F32)
    kap[...] = jnp.zeros_like(kap)
    tl[...] = jnp.zeros_like(tl)
    masks = [block_mask(rt, q, c) for c in range(2)]
    for g in range(NG):
        acc[...] = jnp.zeros_like(acc)
        bbs = [bcc[c * B : (c + 1) * B, g * 128 : (g + 1) * 128] for c in range(2)]
        ccs = [bcc[c * B : (c + 1) * B, 256 + g * 128 : 256 + (g + 1) * 128] for c in range(2)]
        gms = [dnt(ccs[c], bbs[c]) for c in range(2)]

        def tile(jj, carry, g=g, bbs=bbs, ccs=ccs, gms=gms):
            j = g * TPG + jj
            ln = lanes(j)
            e2 = spread_two(j)
            dtte = dnn(mt[:, 0 : 2 * H], e2)
            fs = dnn(mt[:, 2 * H : 4 * H], e2)
            a1 = row_state(later, j, n, 0).astype(F32)
            s0 = row_state(sin, j, n, 0)
            lane = iota((1, 128), 1)
            sk = jnp.where(lane < HEAD_DIM, skip[2 * j], skip[2 * j + 1])
            parts = []
            for c in range(2):
                sl = slice(c * B, (c + 1) * B)
                rb2 = dnn(rs[sl, :], spread_pair(j))
                ls = []
                for i in range(2):
                    h = 2 * j + i
                    lm = jnp.exp(rb2[:, i * B : (i + 1) * B] - r[c, pl.ds(h, 1), :] + masks[c])
                    ls.append(lm * dt[c, pl.ds(h, 1), :])
                xt = xc[sl, ln]
                dyt = dy[sl, ln]
                zero = jnp.zeros_like(dyt)
                dybd = jnp.concatenate(
                    [jnp.where(half, dyt, zero), jnp.where(half, zero, dyt)], axis=0
                )
                dw = dnt(dybd, xt)
                acc[0, c] += dw[0:B] * ls[0] + dw[B : 2 * B] * ls[1]
                wst = jnp.concatenate([(gms[c] * lv).astype(BF16) for lv in ls], axis=0)
                dxw = dtn(wst, dybd)
                if c == 1:
                    ds = a1
                    sp = sb1[:, ln]
                    kk = fs[T - 1 : T]
                else:
                    ds = fs[T - 1 : T] * a1 + dsb1[:, ln].astype(F32)
                    sp = s0
                    kk = fs[B - 1 : B]
                dsh = ds.astype(BF16)
                xf = xt.astype(F32)
                dyf = dyt.astype(F32)
                dtc = dtte[sl]
                dxu = dnn(bbs[c], dsh) * dtc
                uu = (xf * dtc).astype(BF16)
                fd = (fs[sl] * dyf).astype(BF16)
                acc[1, c] += dnt(uu, dsh)
                acc[2, c] += dnt(fd, sp)
                ku = jnp.sum(xf * dxu, axis=0, keepdims=True)
                kd = jnp.sum(ds * sp.astype(F32), axis=0, keepdims=True) * kk
                both = jnp.concatenate(
                    [xf * (dxw + dxu), jnp.broadcast_to(ku + kd, (8, 128))], axis=0
                )
                hs = head_sums(j, both)
                kap[:, sl] += hs[:, 0:B]
                tl[:, c * 8 : (c + 1) * 8] += hs[:, B : B + 8]
                parts.append(dxw + dxu + sk * dyf)
            dxc = jnp.concatenate(parts, axis=0)
            shift_extend(ext, x[:, ln].astype(F32), halo[:, ln].astype(F32))
            own, before, rows = conv_backward(
                ext, vk, live, [cxw[k : k + 1, ln] for k in range(CONV)], cxb[0:1, ln], dxc
            )
            gx_o[:, ln] = own.astype(BF16)
            tail_o[:, ln] = own[T - 16 : T]
            hb_o[:, ln] = before
            for k in range(CONV + 1):
                pk_o[k : k + 1, ln] = rows[k]
            return carry

        lax.fori_loop(0, TPG, tile, 0)
        for c in range(2):
            sl = slice(c * B, (c + 1) * B)
            dg = acc[0, c].astype(BF16)
            dbc[sl, g * 128 : (g + 1) * 128] = acc[1, c] + dtn(dg, ccs[c])
            dbc[sl, 256 + g * 128 : 256 + (g + 1) * 128] = acc[2, c] + dnn(dg, bbs[c])

    for j in range(4):
        sl = slice(j * 128, (j + 1) * 128)
        sd = slice(D + j * 128, D + (j + 1) * 128)
        shift_extend(ext, bc[:, sl].astype(F32), halo[:, sd].astype(F32))
        own, before, rows = conv_backward(
            ext, vk, live, [cbw[k : k + 1, sl] for k in range(CONV)], cbb[0:1, sl], dbc[:, sl]
        )
        gbc_o[:, sl] = own.astype(BF16)
        tail_o[:, sd] = own[T - 16 : T]
        hb_o[:, sd] = before
        for k in range(CONV + 1):
            pk_o[k : k + 1, sd] = rows[k]
    pk_o[5:7, 0:D] = drow[0:2, :]
    pk_o[5:8, D:] = jnp.zeros((3, DB), F32)
    pk_o[7:8, 0:D] = jnp.zeros((1, D), F32)

    rate = jnp.exp(hp[:, 0:1])
    bias = hp[:, 1:2]
    rev = (iota((B, B), 0) >= iota((B, B), 1)).astype(F32)
    rate_sum = jnp.zeros((H, B), F32)
    bias_sum = jnp.zeros((H, B), F32)
    for c in range(2):
        sl = slice(c * B, (c + 1) * B)
        dtv = dt[c]
        kp = kap[:, sl]
        rr = dnn_full(rho[:, sl] - kp, rev) + tl[:, c * 8 : c * 8 + 1]
        ddt = kp / dtv - rate * rr
        gd = ddt * sigmoid(dtr[:, sl].astype(F32) + bias)
        gdt_o[:, sl] = gd
        rate_sum = rate_sum - rate * dtv * rr
        bias_sum = bias_sum + gd
    ones = jnp.ones((8, B), F32)
    zer = jnp.zeros((96, B), F32)
    ph_o[...] = dnt_full(ones, jnp.concatenate([rate_sum, bias_sum, zer[:64]], axis=0))


def param_body(n, pk, ph, hb, red_o, rh_o, own, got, rb, sb, ob, hbuf,
               sd, rd, s1, r1, s2, r2, sh, rh):
    nt = got.shape[0]
    me = lax.axis_index("ctx")
    dp = lax.axis_index("dp")
    ndp = lax.axis_size("dp")
    hbuf[...] = jnp.zeros_like(hbuf)
    barrier = pltpu.get_barrier_semaphore()

    def greet(k, carry):
        pl.semaphore_signal(
            barrier, inc=1, device_id={"ctx": lax.rem(me + k, n)}, device_id_type=MESH
        )
        return carry

    lax.fori_loop(1, n, greet, 0)
    if ndp == 2:
        pl.semaphore_signal(barrier, inc=1, device_id={"dp": 1 - dp}, device_id_type=MESH)
    for j in range(nt - 1):
        own[j] = pk[:, j * 128 : (j + 1) * 128]
    own[nt - 1] = ph[...]
    pl.semaphore_wait(barrier, n - 1 + (ndp - 1))

    def rcopy(src, dst, sem_s, sem_r, dev):
        return pltpu.make_async_remote_copy(
            src_ref=src, dst_ref=dst, send_sem=sem_s, recv_sem=sem_r,
            device_id=dev, device_id_type=MESH,
        )

    back = rcopy(hb, hbuf, sh, rh, {"ctx": lax.rem(me + n - 1, n)})

    @pl.when(me > 0)
    def _():
        back.start()

    if ndp == 2:
        swap = rcopy(own, got, sd, rd, {"dp": 1 - dp})
        swap.start()
        swap.wait()
        sb[...] = own[...] + got[...]
    else:
        sb[...] = own[...]

    def send(k, carry):
        to = lax.rem(me + k, n)

        @pl.when(to < nt)
        def _():
            rcopy(sb.at[to], rb.at[me], s1.at[to], r1.at[me], {"ctx": to}).start()

        return carry

    lax.fori_loop(1, n, send, 0)

    @pl.when(me < nt)
    def _():
        rb[me] = sb[me]

        def collect(d, total):
            @pl.when(d != me)
            def _():
                rcopy(sb.at[0], rb.at[d], s1.at[0], r1.at[d], {"ctx": d}).wait_recv()

            return total + rb[d]

        ob[me] = lax.fori_loop(0, n, collect, jnp.zeros((8, 128), F32))

        def give(k, carry):
            to = lax.rem(me + k, n)
            rcopy(ob.at[me], ob.at[me], s2.at[to], r2.at[me], {"ctx": to}).start()
            return carry

        lax.fori_loop(1, n, give, 0)

    def finish(k, carry):
        d = lax.rem(me + k, n)

        @pl.when(d < nt)
        def _():
            rcopy(sb.at[d], rb.at[0], s1.at[d], r1.at[0], {"ctx": d}).wait_send()
            rcopy(ob.at[0], ob.at[d], s2.at[d], r2.at[d], {"ctx": d}).wait_recv()

        @pl.when(me < nt)
        def _():
            rcopy(ob.at[0], ob.at[0], s2.at[d], r2.at[0], {"ctx": d}).wait_send()

        return carry

    lax.fori_loop(1, n, finish, 0)

    @pl.when(me > 0)
    def _():
        back.wait_send()

    @pl.when(me < n - 1)
    def _():
        back.wait_recv()

    rh_o[...] = hbuf[...]
    red_o[...] = ob[...]


def k5_body(scale, red, rh, tail, flg, gx_in, gbc_in,
            gx_o, gbc_o, cw_o, cb_o, bw_o, bb_o, al_o, db_o, sk_o, ga_o):
    f = flg[:, B:T].astype(F32)
    lane = iota((1, B), 1)
    last = jnp.sum(jnp.where(lane == B - 1, f, 0.0))
    two = jnp.sum(jnp.where(lane >= B - 2, f, 0.0))
    row = iota((16, 128), 0)
    keep = jnp.where(row == 15, 1.0, 0.0)
    keep = keep + jnp.where((row == 14) & (last == 0.0), 1.0, 0.0)
    keep = keep + jnp.where((row == 13) & (two == 0.0), 1.0, 0.0)
    for j in range(NT + 4):
        sl = slice(j * 128, (j + 1) * 128)
        add = jnp.concatenate([jnp.zeros((8, 128), F32), rh[:, sl]], axis=0)
        v = (tail[:, sl] + add * keep).astype(BF16)
        t = red[j] * scale
        if j < NT:
            gx_o[:, sl] = v
            cw_o[:, sl] = t[0:4]
            cb_o[:, sl] = t[4:5]
            ga_o[:, sl] = t[5:6]
            hs = dnt_full(t[0:8], collect_two(j).astype(F32))
            if j == 0:
                skip = hs
            else:
                skip = skip + hs
        else:
            so = slice(j * 128 - D, (j + 1) * 128 - D)
            gbc_o[:, so] = v
            bw_o[:, so] = t[0:4]
            bb_o[:, so] = t[4:5]
    sk_o[...] = skip[6:7]
    last_tile = red[NT + 4] * scale
    al_o[...] = last_tile[0:1, 0:H]
    db_o[...] = last_tile[0:1, H : 2 * H]


def sds(*shape, dtype=F32):
    return jax.ShapeDtypeStruct(shape, dtype)


def call(body, outs, ins, scratch=(), specs=None, out_specs=None, cid=None, **kw):
    extra = {} if cid is None else {"collective_id": cid, "has_side_effects": True}
    return pl.pallas_call(
        body,
        out_shape=outs,
        in_specs=specs or [VM] * len(ins),
        out_specs=out_specs or [VM] * len(outs),
        scratch_shapes=list(scratch),
        compiler_params=pltpu.CompilerParams(vmem_limit_bytes=VLIM, **extra),
        **kw,
    )(*ins)


def per_device(
    x_raw, bc_raw, z_gate, dt_raw, resets, conv_x_weight, conv_x_bias, conv_bc_weight,
    conv_bc_bias, a_log, dt_bias, skip_weight, norm_gain, grad_out,
):
    n = lax.axis_size("ctx")
    nh = lax.axis_size("head")
    ndp = lax.axis_size("dp")
    ncq = n // 8
    w = D // ncq
    x = x_raw[0]
    bc = bc_raw[0].reshape(T, DB)
    z = z_gate[0]
    go = grad_out[0]
    dtr = dt_raw[0]
    gain = norm_gain.reshape(1, D)
    cxb = conv_x_bias.reshape(1, D)
    cbw = conv_bc_weight.reshape(CONV, DB)
    cbb = conv_bc_bias.reshape(1, DB)
    hp = jnp.stack([a_log, dt_bias], axis=1)

    f = resets[0, T - 8 :]
    keep = jnp.concatenate([jnp.cumsum(f[::-1])[::-1][1:] == 0, jnp.ones((1,), bool)])
    tail = jnp.concatenate([x[T - 8 :], bc[T - 8 :]], axis=1)
    tail = jnp.where(keep[:, None], tail, jnp.zeros_like(tail))
    halo = lax.ppermute(tail, "ctx", [(i, i + 1) for i in range(n - 1)])

    conv_scratch = [
        pltpu.VMEM((T + 8, 128), F32),
        pltpu.VMEM((T + 8, 128), F32),
        pltpu.VMEM((CONV - 1, T, 128), F32),
    ]
    xc, bcc, dt, r, mt, rt, rs, q, st, kr, fr = call(
        functools.partial(k1_body, n),
        (
            sds(T, D, dtype=BF16), sds(T, DB, dtype=BF16), sds(2, H, B), sds(2, H, B),
            sds(T, 128, dtype=BF16), sds(T, 128), sds(T, 128, dtype=BF16), sds(8, T),
            sds(n, ROWS, w, dtype=BF16), sds(ncq, 1, w), sds(NSTATE, D),
        ),
        (x, bc, halo, dtr, resets, hp, conv_x_weight, cxb, cbw, cbb),
        conv_scratch,
    )
    state = pltpu.VMEM((n, ROWS, w), BF16)
    dma = pltpu.SemaphoreType.DMA((n,))
    sin, kall = call(
        functools.partial(scan_body, n, True),
        (sds(n, ROWS, w, dtype=BF16), sds(n, 1, w)),
        (st, kr),
        [state, state, state, pltpu.VMEM((n, 1, w), F32)] + [dma] * 6,
        cid=0,
    )
    y, mixed, sums, sb1 = call(
        functools.partial(k2_body, n),
        (sds(T, D), sds(T, D, dtype=BF16), sds(16, T), sds(NSTATE, D, dtype=BF16)),
        (xc, bcc, dt, r, rt, rs, mt, q, sin, fr, z, go, gain, skip_weight),
        [pltpu.VMEM((2, T, 128), F32)],
        specs=[VM] * 13 + [SM],
    )
    if nh > 1:
        (sums,) = call(
            functools.partial(norm_body, nh),
            (sds(16, T),),
            (sums,),
            [pltpu.VMEM((nh, 16, T), F32)] + [pltpu.SemaphoreType.DMA((nh,))] * 2,
            cid=1,
        )
    dz, dy, rho, drow, ad, dsb1 = call(
        functools.partial(k3_body, n),
        (
            sds(T, D, dtype=BF16), sds(T, D, dtype=BF16), sds(H, T), sds(8, D),
            sds(n, ROWS, w, dtype=BF16), sds(NSTATE, D, dtype=BF16),
        ),
        (sums, mixed, z, go, gain, y, xc, mt, bcc),
        [pltpu.VMEM((T, 128), F32)] * 2,
    )
    (later,) = call(
        functools.partial(scan_body, n, False),
        (sds(n, ROWS, w, dtype=BF16),),
        (ad, kall),
        [state, state, state] + [dma] * 4,
        cid=2,
    )
    gx, gbc, gdt, tails, hb, pk, ph = call(
        functools.partial(k4_body, n),
        (
            sds(T, D, dtype=BF16), sds(T, DB, dtype=BF16), sds(H, T), sds(16, D + DB),
            sds(8, D + DB), sds(8, D + DB), sds(8, 128),
        ),
        (
            x, bc, halo, dtr, hp, conv_x_weight, cxb, cbw, cbb, xc, bcc, dt, r, rt, rs, mt, q,
            dy, rho, dsb1, sin, sb1, later, drow, skip_weight,
        ),
        conv_scratch
        + [
            pltpu.VMEM((CONV, T + 16, 128), F32),
            pltpu.VMEM((3, 2, B, 128), F32),
            pltpu.VMEM((H, T), F32),
            pltpu.VMEM((H, 16), F32),
            pltpu.VMEM((T, DB), F32),
        ],
        specs=[VM] * 24 + [SM],
    )
    nt = NT + 5
    owners = pltpu.SemaphoreType.DMA((max(n, nt),))
    one = pltpu.SemaphoreType.DMA
    tiles = pltpu.VMEM((nt, 8, 128), F32)
    red, rh = call(
        functools.partial(param_body, n),
        (sds(nt, 8, 128), sds(8, D + DB)),
        (pk, ph, hb),
        [tiles, tiles, pltpu.VMEM((n, 8, 128), F32), tiles, tiles, pltpu.VMEM((8, D + DB), F32)]
        + [one, one] + [owners] * 4 + [one, one],
        cid=3,
    )
    scale = float(ndp * n * T) ** (-0.5)
    whole = lambda *s: pl.BlockSpec(s, lambda i: (0,) * len(s))
    outs = pl.pallas_call(
        functools.partial(k5_body, scale),
        grid=(1,),
        out_shape=(
            sds(T, D, dtype=BF16), sds(T, DB, dtype=BF16), sds(CONV, D), sds(1, D), sds(CONV, DB),
            sds(1, DB), sds(1, H), sds(1, H), sds(1, H), sds(1, D),
        ),
        in_specs=[
            whole(nt, 8, 128), whole(8, D + DB), whole(16, D + DB), whole(1, T),
            pl.BlockSpec(memory_space=pl.ANY), pl.BlockSpec(memory_space=pl.ANY),
        ],
        out_specs=[
            pl.BlockSpec((16, D), lambda i: (T // 16 - 1, 0)),
            pl.BlockSpec((16, DB), lambda i: (T // 16 - 1, 0)),
            whole(CONV, D), whole(1, D), whole(CONV, DB), whole(1, DB), whole(1, H), whole(1, H),
            whole(1, H), whole(1, D),
        ],
        input_output_aliases={4: 0, 5: 1},
    )(red, rh, tails, resets, gx, gbc)
    gx, gbc, cw, cb, bw, bb, al, db, sk, ga = outs
    return (
        gx[None], gbc.reshape(1, T, 2, DB // 2), dz[None], gdt[None], cw, cb.reshape(D),
        bw.reshape(CONV, 2, DB // 2), bb.reshape(2, DB // 2), al.reshape(H), db.reshape(H),
        sk.reshape(H), ga.reshape(D),
    )


def solution(mesh):
    return jax.shard_map(
        per_device,
        mesh=mesh,
        in_specs=(
            P("dp", "ctx", "head"),
            P("dp", "ctx", None, "head"),
            P("dp", "ctx", "head"),
            P("dp", "head", "ctx"),
            P("dp", "ctx"),
            P(None, "head"),
            P("head"),
            P(None, None, "head"),
            P(None, "head"),
            P("head"),
            P("head"),
            P("head"),
            P("head"),
            P("dp", "ctx", "head"),
        ),
        out_specs=(
            P("dp", "ctx", "head"),
            P("dp", "ctx", None, "head"),
            P("dp", "ctx", "head"),
            P("dp", "head", "ctx"),
            P(None, "head"),
            P("head"),
            P(None, None, "head"),
            P(None, "head"),
            P("head"),
            P("head"),
            P("head"),
            P("head"),
        ),
        check_vma=False,
    )
```

time: 1200 us -> 181 us (0.15)
  the two profiles are of different devices: /device:TPU:128 before, /device:TPU:1 now
where the time goes in v1:
time: 181 us; the launch traced here: 180 us
  Pallas kernels  161 us (89%)
  local copies, waits for them, and re-layouts  12.1 us (7%)
  starting transfers between devices  4.02 us (2%)
  other arithmetic  2.34 us (1%)
    pallas_call x8, Pallas kernels, call(): pl.pallas_call(body, out_shape=outs, in_specs=specs or [VM] * len(ins), o...  159 us
    unnamed x7, local copies, waits for them, and re-layouts  5.55 us
    ppermute x1, starting transfers between devices, per_device(): halo = lax.ppermute(tail, 'ctx', [(i, i + 1) for i in range(n - 1)])  4.02 us
  transfers between devices with their start and end apart: 1, of which 0 were waited for; matrix products, arithmetic and copies ran while one was open for 3% of the time, Pallas kernels for 0%

profile of v1, /device:TPU:1, one launch (start us, length us, event | category | flops | bytes accessed | tf_op | source)
XLA Modules:
  0.0 180.4 jit_solution(15604352682695193250)
XLA Ops:
  0.6 0.8 slice_bitcast_fusion
  1.4 0.7 slice_bitcast_fusion.1
  2.1 0.7 slice_bitcast_fusion.3
  3.4 4.0 %collective-permute-start = (bf16[8,2560]{1,0:T(8,128)(2,1)S(1)}, bf16[8,2560]{1,0:T(8,128)(2,1)S(1)}, u32[]{:S(2)}, u32[]{:S(2)}) collective-permute-start(bf16[8,2560]{1,0:T(8,128)(2,1)S(1)} %maximum_select_fusion), channel_id=1, source_target_pairs={{0,4},{4,8},{8,12},{12,16},{16,20},{20,24},{24,28},{28,32},{32,36}... | collective-permute-start | bytes 122888 | tf_op jit(solution)/shard_map/ppermute | solution.py:751
  7.4 0.7 pad_maximum_fusion
  8.1 1.7 copy.32
  9.8 0.7 copy.31.hp
  10.5 1.3 copy.34
  11.8 1.3 copy.35
  13.0 0.6 copy-done
  13.6 8.8 %shard_map.229 = (bf16[256,2048]{1,0:T(8,128)(2,1)}, bf16[256,512]{1,0:T(8,128)(2,1)}, f32[2,32,128]{2,1,0:T(8,128)}, f32[2,32,128]{2,1,0:T(8,128)}, bf16[256,12...) custom-call(bf16[256,2048]{1,0:T(8,128)(2,1)} %bitcast.35, ...), custom_call_target="tpu_custom_call" | custom-call | tf_op jit(solution)/shard_map/pallas_call | solution.py:716
  22.5 33.0 %shard_map.230 = (bf16[32,16,512]{2,1,0:T(8,128)(2,1)}, f32[32,1,512]{2,1,0:T(1,128)}) custom-call(bf16[32,16,512]{2,1,0:T(8,128)(2,1)} %get-tuple-element.62.refs_0_, f32[4,1,512]{2,1,0:T(1,128)} %get-tuple-element.63.refs_1_), custom_call_target="tpu_custom_call" | custom-call | tf_op jit(solution)/shard_map/pallas_call | solution.py:716
  55.4 15.6 %shard_map.231 = (f32[256,2048]{1,0:T(8,128)}, bf16[256,2048]{1,0:T(8,128)(2,1)}, f32[16,256]{1,0:T(8,128)}, bf16[128,2048]{1,0:T(8,128)(2,1)}) custom-call(bf16[256,2048]{1,0:T(8,128)(2,1)} %get-tuple-element.54.xc, bf16[256,512]{1,0:T(8,128)(2,1)} %get-tuple-element.55.bcc, f32[2,32,128]{2,1,0:T(8,128)} %get-tuple-element.56.dt, ...), custom_call_target="tpu_custom_call" | custom-call | tf_op jit(solution)/shard_map/pallas_call | solution.py:716
  71.1 6.4 %shard_map.232.sums = f32[16,256]{1,0:T(8,128)} custom-call(f32[16,256]{1,0:T(8,128)} %get-tuple-element.66.s_in), custom_call_target="tpu_custom_call" | custom-call | tf_op jit(solution)/shard_map/pallas_call | solution.py:716
  77.5 10.6 %shard_map.233 = (bf16[256,2048]{1,0:T(8,128)(2,1)}, bf16[256,2048]{1,0:T(8,128)(2,1)}, f32[32,256]{1,0:T(8,128)}, f32[8,2048]{1,0:T(8,128)}, bf16[32,16,512]{2,1,0:T(8,128)(2,1)}, /*index=5*/bf16[128,2048]{1,0:T(8,128)(2,1)}) custom-call(f32[16,256]{1,0:T(8,128)} %shard_map.232.sums, bf16[256,2048]{1,0:T(8,128)(2,1)} %get-tuple-element.67.mixed, ...), custom_call_target="tpu_custom_call" | custom-call | tf_op jit(solution)/shard_map/pallas_call | solution.py:716
  88.0 39.6 %shard_map.234.later = bf16[32,16,512]{2,1,0:T(8,128)(2,1)} custom-call(bf16[32,16,512]{2,1,0:T(8,128)(2,1)} %get-tuple-element.73.refs_0_, f32[32,1,512]{2,1,0:T(1,128)} %get-tuple-element.74.refs_1_), custom_call_target="tpu_custom_call" | custom-call | tf_op jit(solution)/shard_map/pallas_call | solution.py:716
  127.7 21.1 %shard_map.235 = (bf16[256,2048]{1,0:T(8,128)(2,1)}, bf16[256,512]{1,0:T(8,128)(2,1)}, f32[32,256]{1,0:T(8,128)}, f32[16,2560]{1,0:T(8,128)}, f32[8,2560]{1,0:T(...) custom-call(bf16[256,2048]{1,0:T(8,128)(2,1)} %bitcast.36, bf16[256,512]{1,0:T(8,128)(2,1)} %bitcast.42, ...), custom_call_target="tpu_custom_call" | custom-call | tf_op jit(solution)/shard_map/pallas_call | solution.py:716
  148.8 23.9 %shard_map.236 = (f32[21,8,128]{2,1,0:T(8,128)}, f32[8,2560]{1,0:T(8,128)}) custom-call(f32[8,2560]{1,0:T(8,128)} %get-tuple-element.76.pk, f32[8,128]{1,0:T(8,128)} %get-tuple-element.77.ph, f32[8,2560]{1,0:T(8,128)} %get-tuple-element.78.hb), custom_call_target="tpu_custom_call" | custom-call | tf_op jit(solution)/shard_map/pallas_call | solution.py:716
  172.8 2.1 %shard_map.237 = (bf16[256,2048]{1,0:T(8,128)(2,1)}, bf16[256,512]{1,0:T(8,128)(2,1)}, f32[4,2048]{1,0:T(4,128)}, f32[1,2048]{1,0:T(1,128)}, f32[4,512]{1,0:T(4,...) custom-call(f32[21,8,128]{2,1,0:T(8,128)} %get-tuple-element.79.red,, ...), custom_call_target="tpu_custom_call", output_to_operand_aliasing={{0}: (4, {}), {1}: (5, {})} | custom-call | tf_op jit(solution)/shard_map/pallas_call | solution.py:842
  174.9 1.7 reshape.78
  176.6 1.3 reshape.80
  177.9 0.5 broadcast.9
  178.5 1.3 reduce.3
  179.8 0.6 reshape.81
  (10 shorter events, 0.6 us)
Async XLA Ops:
  3.4 9.6 %collective-permute-start = (bf16[8,2560]{1,0:T(8,128)(2,1)S(1)}, bf16[8,2560]{1,0:T(8,128)(2,1)S(1)}, u32[]{:S(2)}, u32[]{:S(2)}) collective-permute-start(bf16[8,2560]{1,0:T(8,128)(2,1)S(1)} %maximum_select_fusion), channel_id=1, source_target_pairs={{0,4},{4,8},{8,12},{12,16},{16,20},{20,24},{24,28},{28,32},{32,36}... | collective-permute-start | bytes 122888 | tf_op jit(solution)/shard_map/ppermute | solution.py:751
  13.0 0.6 copy-start

commit v2 on v0

v2 whole, which is shorter than its diff:
```python
import functools

import types

import jax
import jax.numpy as jnp
from jax import lax
from jax.experimental import pallas as pl
from jax.experimental.pallas import tpu as pltpu
from jax.sharding import PartitionSpec as P

F32 = jnp.float32
BF16 = jnp.bfloat16
HIGHEST = lax.Precision.HIGHEST
MESH = pl.DeviceIdType.MESH

HEAD_DIM = 64
NSTATE = 128
CONV = 4
INNER = 8192
EPS = 1e-05

T = 256
B = 128
H = 32
D = 2048
DB = 512
NT = D // 128
NG = 2
TPG = NT // NG
ROWS = 16
VM = pl.BlockSpec(memory_space=pltpu.VMEM)
SM = pl.BlockSpec(memory_space=pltpu.SMEM)
VLIM = 60 * 1024 * 1024


def dnn(a, b):
    return lax.dot_general(a, b, (((1,), (0,)), ((), ())), preferred_element_type=F32)


def dnt(a, b):
    return lax.dot_general(a, b, (((1,), (1,)), ((), ())), preferred_element_type=F32)


def dtn(a, b):
    return lax.dot_general(a, b, (((0,), (0,)), ((), ())), preferred_element_type=F32)


def dnn_full(a, b):
    return lax.dot_general(
        a, b, (((1,), (0,)), ((), ())), precision=HIGHEST, preferred_element_type=F32
    )


def dnt_full(a, b):
    return lax.dot_general(
        a, b, (((1,), (1,)), ((), ())), precision=HIGHEST, preferred_element_type=F32
    )


def iota(shape, dim):
    return lax.broadcasted_iota(jnp.int32, shape, dim)


def high_low(v):
    high = v.astype(BF16).astype(F32)
    return high, v - high


def sigmoid(v):
    return 1.0 / (1.0 + jnp.exp(-v))


def softplus(v):
    y = jnp.exp(-jnp.abs(v))
    series = y * (1.0 - y * (0.5 - y * (1.0 / 3.0 - y * (0.25 - 0.2 * y))))
    return jnp.maximum(v, 0.0) + jnp.where(y < 0.02, series, jnp.log(1.0 + y))


def lanes(j):
    return pl.ds(pl.multiple_of(j * 128, 128), 128)


def spread_two(j):
    row = iota((2 * H, 128), 0) % H
    lane = iota((2 * H, 128), 1)
    return (row == 2 * j + lane // HEAD_DIM).astype(BF16)


def spread_pair(j):
    row = iota((128, 256), 0)
    lane = iota((128, 256), 1)
    return ((row % H == 2 * j + lane // 128) & (row < 3 * H)).astype(BF16)


def collect_two(j):
    row = iota((H, 128), 0)
    lane = iota((H, 128), 1)
    return (row == 2 * j + lane // HEAD_DIM).astype(BF16)


def head_sums(j, v):
    high = v.astype(BF16)
    low = (v - high.astype(F32)).astype(BF16)
    e = collect_two(j)
    return dnt(e, high) + dnt(e, low)


def conv_input(ext, live, w, bias, lo, rows):
    u = bias + w[0] * ext[8 + lo : 8 + lo + rows, :]
    for k in range(1, CONV):
        u = u + w[k] * ext[8 - k + lo : 8 - k + lo + rows, :] * live[k - 1, lo : lo + rows, :]
    return u


def live_masks(cnt, live):
    now = cnt[8 : 8 + T, :]
    for k in range(1, CONV):
        live[k - 1] = (now == cnt[8 - k : 8 - k + T, :]).astype(F32)


def block_mask(rt, q, c):
    qc = rt[c * B : (c + 1) * B, H : H + 1]
    qr = q[0:1, c * B : (c + 1) * B]
    ok = (qc == qr) & (iota((B, B), 0) >= iota((B, B), 1))
    return jnp.where(ok, 0.0, -1e30)


def row_state(ref, j, n, lead):
    ncq = n // 8
    tpc = NT // ncq
    cq = j // tpc
    lane = lanes(j % tpc)
    return jnp.concatenate([ref[rz * ncq + cq, :, lane] for rz in range(8)], axis=0)


def put_state(ref, j, n, v):
    ncq = n // 8
    tpc = NT // ncq
    cq = j // tpc
    lane = lanes(j % tpc)
    for rz in range(8):
        ref[rz * ncq + cq, :, lane] = v[rz * ROWS : (rz + 1) * ROWS]


def column(row):
    return jnp.concatenate(
        [jnp.broadcast_to(row, (128, H)), jnp.zeros((128, 128 - H), F32)], axis=1
    ).T[0:H, 0:1]


def rcopy(src, dst, sem_s, sem_r, dev):
    return pltpu.make_async_remote_copy(
        src_ref=src, dst_ref=dst, send_sem=sem_s, recv_sem=sem_r,
        device_id=dev, device_id_type=MESH,
    )


def send_pieces(n, st, rb, s1, r1, cq, me):
    ncq = n // 8

    def send(rz, carry):
        to = rz * ncq + cq

        @pl.when(to != me)
        def _():
            rcopy(st.at[to], rb.at[me], s1.at[to], r1.at[me], {"ctx": to}).start()

        return carry

    lax.fori_loop(0, 8, send, 0)


def owner_scan(n, st, rb, pb, ob, kb, s1, r1, s2, r2, me, backward):
    rb[me] = st[me]

    def step(i, acc):
        d = n - 1 - i if backward else i

        @pl.when(d != me)
        def _():
            rcopy(st.at[0], rb.at[d], s1.at[d], r1.at[d], {"ctx": d}).wait_recv()

        pb[d] = acc.astype(BF16)

        @pl.when(d != me)
        def _():
            rcopy(pb.at[d], ob.at[me], s2.at[d], r2.at[me], {"ctx": d}).start()

        return kb[d] * acc + rb[d].astype(F32)

    lax.fori_loop(0, n, step, jnp.zeros(rb.shape[1:], F32))
    ob[me] = pb[me]


def take_pieces(n, pb, ob, s2, r2, me):
    def step(k, carry):
        d = lax.rem(me + k, n)
        rcopy(pb.at[d], ob.at[d], s2.at[d], r2.at[d], {"ctx": d}).wait_recv()
        return carry

    lax.fori_loop(1, n, step, 0)


def main_body(n, nh, ndp, nt, names, *refs):
    r = types.SimpleNamespace(**dict(zip(names, refs)))
    ncq = n // 8
    tpc = NT // ncq
    me = lax.axis_index("ctx")
    dp = lax.axis_index("dp")
    hd = lax.axis_index("head")
    ne = n * ndp
    mine = dp * n + me
    half = iota((B, 128), 1) < HEAD_DIM
    lane1 = iota((1, 128), 1)
    blocks = [slice(0, B), slice(B, T)]

    r.hbuf[...] = jnp.zeros_like(r.hbuf)
    r.bbuf[...] = jnp.zeros_like(r.bbuf)
    barrier = pltpu.get_barrier_semaphore()

    def greet(k, carry):
        e = lax.rem(mine + k, ne)
        pl.semaphore_signal(
            barrier, inc=1, device_id={"dp": e // n, "ctx": lax.rem(e, n)}, device_id_type=MESH
        )
        return carry

    lax.fori_loop(1, ne, greet, 0)
    for k in range(1, nh):
        pl.semaphore_signal(
            barrier, inc=1, device_id={"head": lax.rem(hd + k, nh)}, device_id_type=MESH
        )
    zcopy = pltpu.make_async_copy(r.z_hbm.at[0], r.z, r.zs)
    gcopy = pltpu.make_async_copy(r.go_hbm.at[0], r.go, r.gs)
    zcopy.start()
    gcopy.start()

    rate = jnp.exp(column(r.alog[...]))
    bias = column(r.dtb[...])
    tri = (iota((B, B), 0) <= iota((B, B), 1)).astype(F32)
    before = jnp.zeros((8, 1), F32)
    r.cnt[0:8, :] = jnp.zeros((8, 128), F32)
    masks = []
    for c in range(2):
        sl = blocks[c]
        dtv = softplus(r.dtr[0, :, sl].astype(F32) + bias)
        run = dnn_full(-rate * dtv, tri)
        q = dnn(jnp.broadcast_to(r.flg[:, sl].astype(F32), (8, B)), tri)
        rl = run[:, B - 1 : B]
        ql = q[:, B - 1 : B]
        dtte = dtv * jnp.where(q[0:1] == ql[0:1], jnp.exp(rl - run), 0.0)
        fs = jnp.where(q[0:1] == 0.0, jnp.exp(run), 0.0)
        r.dt[c] = dtv
        r.run[c] = run
        a1, a2 = high_low(dtte)
        b1, b2 = high_low(fs)
        r.mt[sl, :] = jnp.concatenate([a1, a2, b1, b2], axis=0).T.astype(BF16)
        dev = q + before
        before = dev[:, B - 1 : B]
        rt = jnp.concatenate([q, dev, jnp.zeros((112, B), F32)], axis=0).T
        r1, r2 = high_low(run)
        r2, r3 = high_low(r2)
        r.rs[sl, :] = jnp.concatenate(
            [r1, r2, r3, jnp.zeros((H, B), F32)], axis=0
        ).T.astype(BF16)
        r.cnt[8 + c * B : 8 + (c + 1) * B, :] = jnp.broadcast_to(rt[:, 8:9], (B, 128))
        ok = (rt[:, 0:1] == q[0:1, :]) & (iota((B, B), 0) >= iota((B, B), 1))
        r.mask[c] = jnp.where(ok, 0.0, -1e30)
    live_masks(r.cnt, r.live)

    row16 = iota((16, 128), 0)
    same = (r.cnt[8 + T - 16 : 8 + T, :] == r.cnt[8 + T - 1 : 8 + T, :])
    for j in range(NT + 4):
        v = r.x[0, T - 16 : T, j * 128 : (j + 1) * 128] if j < NT else r.bc[
            T - 16 : T, j * 128 - D : (j + 1) * 128 - D
        ]
        r.tail[:, j * 128 : (j + 1) * 128] = jnp.where(same, v.astype(F32), 0.0).astype(BF16)

    def bc_weights(j):
        i, sl = j // 2, slice((j % 2) * 128, (j % 2) * 128 + 128)
        return [r.cbw[k, i : i + 1, sl] for k in range(CONV)], r.cbb[i : i + 1, sl]

    def x_weights(ln):
        return [r.cxw[k : k + 1, ln] for k in range(CONV)], r.cxb[0:1, ln]

    def bc_conv(c):
        for j in range(4):
            sl = slice(j * 128, (j + 1) * 128)
            ext = r.ext.at[j]
            if c == 1:
                ext[8 : 8 + T, :] = r.bc[:, sl].astype(F32)
            else:
                ext[8 : 8 + B, :] = r.bc[0:B, sl].astype(F32)
                ext[0:8, :] = r.hbuf[8:16, D + j * 128 : D + (j + 1) * 128].astype(F32)
            u = conv_input(ext, r.live, *bc_weights(j), c * B, B)
            sg = sigmoid(u)
            r.bcc[blocks[c], sl] = (u * sg).astype(BF16)
            r.cdb[blocks[c], sl] = sg * (1.0 + u * (1.0 - sg))

    def x_conv(j, c):
        ln = lanes(j)
        ext = r.ext.at[j % 4]
        if c == 1:
            ext[8 : 8 + T, :] = r.x[0, :, ln].astype(F32)
        else:
            ext[8 : 8 + B, :] = r.x[0, 0:B, ln].astype(F32)
            ext[0:8, :] = r.hbuf[8:16, ln].astype(F32)
        u = conv_input(ext, r.live, *x_weights(ln), c * B, B)
        xc = (u * sigmoid(u)).astype(BF16)
        r.xc[blocks[c], ln] = xc
        dtte = dnn(r.mt[blocks[c], 0 : 2 * H], spread_two(j))
        return (xc.astype(F32) * dtte).astype(BF16)

    def b_turned(g, c):
        return r.bcc[blocks[c], g * 128 : (g + 1) * 128].astype(F32).T.astype(BF16)

    def keep_row(j, c):
        return dnn(r.mt[(c + 1) * B - 16 : (c + 1) * B, 2 * H : 4 * H], spread_two(j))[15:16]

    bc_conv(1)
    for g in range(NG):
        bt = b_turned(g, 1)

        def second(jj, carry, g=g, bt=bt):
            j = g * TPG + jj
            r.fr[1, :, lanes(j)] = dnn(bt, x_conv(j, 1))
            return carry

        lax.fori_loop(0, TPG, second, 0, unroll=2)
        if g == 0:
            pl.semaphore_wait(barrier, ne - 1 + nh - 1)
            halo = rcopy(r.tail, r.hbuf, r.sh, r.rh, {"ctx": lax.rem(me + 1, n)})

            @pl.when(me < n - 1)
            def _():
                halo.start()

    @pl.when(me > 0)
    def _():
        halo.wait_recv()

    bc_conv(0)
    bts = [b_turned(g, 0) for g in range(NG)]
    for cq in range(ncq):
        bt = bts[cq * tpc // TPG]

        def first(jj, carry, cq=cq, bt=bt):
            j = cq * tpc + jj
            ln = lanes(j)
            fresh = dnn(bt, x_conv(j, 0))
            r.fr[0, :, ln] = fresh
            k1 = keep_row(j, 1)
            put_state(r.st, j, n, (k1 * fresh + r.fr[1, :, ln]).astype(BF16))
            r.kr[cq, :, lanes(jj)] = keep_row(j, 0) * k1
            return carry

        lax.fori_loop(0, tpc, first, 0, unroll=2)
        send_pieces(n, r.st, r.rb, r.s1, r.r1, cq, me)

        def send_row(rz, carry, cq=cq):
            to = rz * ncq + cq

            @pl.when(to != me)
            def _():
                rcopy(r.kr.at[cq], r.kb.at[me], r.sk.at[to], r.rk.at[me], {"ctx": to}).start()

            return carry

        lax.fori_loop(0, 8, send_row, 0)

    def group_parts(g, c):
        return (
            r.bcc[blocks[c], g * 128 : (g + 1) * 128],
            r.bcc[blocks[c], 256 + g * 128 : 256 + (g + 1) * 128],
        )

    for g in range(NG):
        for c in range(2):
            bb, cc = group_parts(g, c)
            r.gm[...] = dnt(cc, bb)

            def inside(jj, carry, g=g, c=c):
                j = g * TPG + jj
                ln = lanes(j)
                rb2 = dnn(r.rs[blocks[c], :], spread_pair(j))
                ws = []
                for i in range(2):
                    h = 2 * j + i
                    lm = jnp.exp(
                        rb2[:, i * B : (i + 1) * B] - r.run[c, pl.ds(h, 1), :] + r.mask[c]
                    ) * r.dt[c, pl.ds(h, 1), :]
                    r.lm[2 * j + c, i * B : (i + 1) * B, :] = lm
                    wv = (r.gm[...] * lm).astype(BF16)
                    r.wm[2 * j + c, i * B : (i + 1) * B, :] = wv
                    ws.append(wv)
                xt = r.xc[blocks[c], ln]
                zero = jnp.zeros_like(xt)
                xbd = jnp.concatenate(
                    [jnp.where(half, xt, zero), jnp.where(half, zero, xt)], axis=0
                )
                r.y[blocks[c], ln] = dnn(jnp.concatenate(ws, axis=1), xbd)
                return carry

            lax.fori_loop(0, TPG, inside, 0, unroll=2)

    r.kb[me] = r.kr[lax.rem(me, ncq)]

    def rows_in(k, carry):
        d = lax.rem(me + k, n)
        rcopy(r.kr.at[0], r.kb.at[d], r.sk.at[d], r.rk.at[d], {"ctx": d}).wait_recv()
        return carry

    lax.fori_loop(1, n, rows_in, 0)
    owner_scan(n, r.st, r.rb, r.pb, r.ob, r.kb, r.s1, r.r1, r.s2, r.r2, me, False)

    zcopy.wait()
    gcopy.wait()

    def prepare(j, carry):
        ln = lanes(j)
        zf = r.z[:, ln].astype(F32)
        sg = sigmoid(zf)
        r.gate[:, ln] = zf * sg
        r.dgate[:, ln] = sg * (1.0 + zf * (1.0 - sg))
        ext = r.ext.at[j % 4]
        ext[8 : 8 + T, :] = r.x[0, :, ln].astype(F32)
        ext[0:8, :] = r.hbuf[8:16, ln].astype(F32)
        for c in range(2):
            u = conv_input(ext, r.live, *x_weights(ln), c * B, B)
            sg = sigmoid(u)
            r.cdx[blocks[c], ln] = sg * (1.0 + u * (1.0 - sg))
        return carry

    lax.fori_loop(0, NT, prepare, 0)
    take_pieces(n, r.pb, r.ob, r.s2, r.r2, me)

    r.sums_acc[...] = jnp.zeros_like(r.sums_acc)

    def skip_row(j):
        return jnp.where(lane1 < HEAD_DIM, r.skip[2 * j], r.skip[2 * j + 1])

    for g in range(NG):
        ccs = [group_parts(g, c)[1] for c in range(2)]

        def outputs(jj, carry, g=g, ccs=ccs):
            j = g * TPG + jj
            ln = lanes(j)
            fs = dnn(r.mt[:, 2 * H : 4 * H], spread_two(j))
            sb0 = row_state(r.ob, j, n, 0)
            sb1 = (fs[B - 1 : B] * sb0.astype(F32) + r.fr[0, :, ln]).astype(BF16)
            r.sb1[:, ln] = sb1
            for c in range(2):
                sl = blocks[c]
                y = r.y[sl, ln] + dnn(ccs[c], sb0 if c == 0 else sb1) * fs[sl]
                r.y[sl, ln] = y
                mixed = (y + skip_row(j) * r.xc[sl, ln].astype(F32)).astype(BF16)
                r.mixed[sl, ln] = mixed
                gated = mixed.astype(F32) * r.gate[sl, ln]
                gained = r.go[sl, ln].astype(F32) * r.gain[0:1, ln]
                r.sums_acc[0, sl, :] += gated * gated
                r.sums_acc[1, sl, :] += gated * gained
            return carry

        lax.fori_loop(0, TPG, outputs, 0, unroll=2)
    ones = jnp.ones((8, 128), F32)
    r.sums[0:8, :] = dnt_full(ones, r.sums_acc[0])
    r.sums[8:16, :] = dnt_full(ones, r.sums_acc[1])
    copies = []
    for k in range(1, nh):
        copies.append(
            rcopy(r.sums, r.sbuf.at[k], r.hs.at[k], r.hr.at[k], {"head": lax.rem(hd + k, nh)})
        )
        copies[-1].start()
    for cp in copies:
        cp.wait()
    parts = [r.sums[...]] + [r.sbuf[k] for k in range(1, nh)]
    total = jnp.zeros_like(parts[0])
    for d in range(nh):
        for k in range(nh):
            total = total + jnp.where(lax.rem(hd - k + nh, nh) == d, parts[k], 0.0)
    inv = lax.rsqrt(total[0:8] / INNER + EPS)
    coef = inv * inv * inv * total[8:16] / INNER
    for c in range(2):
        sl = blocks[c]
        tr = jnp.concatenate([inv[:, sl], coef[:, sl], jnp.zeros((112, B), F32)], axis=0).T
        r.inv[sl, :] = jnp.broadcast_to(tr[:, 0:1], (B, 128))
        r.coef[sl, :] = jnp.broadcast_to(tr[:, 8:9], (B, 128))

    r.rho[...] = jnp.zeros_like(r.rho)
    r.skc[...] = jnp.zeros_like(r.skc)
    cts = [[group_parts(g, c)[1].astype(F32).T.astype(BF16) for c in range(2)] for g in range(NG)]
    for cq in range(ncq):
        ct = cts[cq * tpc // TPG]

        def gates(jj, carry, cq=cq, ct=ct):
            j = cq * tpc + jj
            ln = lanes(j)
            e2 = spread_two(j)
            grow = jnp.zeros((1, 128), F32)
            srow = jnp.zeros((1, 128), F32)
            ds = []
            for c in range(2):
                sl = blocks[c]
                m = r.mixed[sl, ln].astype(F32)
                gt = r.gate[sl, ln]
                go = r.go[sl, ln].astype(F32)
                gated = m * gt
                iv = r.inv[sl, :]
                dg = go * r.gain[0:1, ln] * iv - gated * r.coef[sl, :]
                grow = grow + jnp.sum(go * gated * iv, axis=0, keepdims=True)
                r.dz[sl, ln] = (dg * m * r.dgate[sl, ln]).astype(BF16)
                dm = (dg * gt).astype(BF16)
                r.dy[sl, ln] = dm
                dy = dm.astype(F32)
                srow = srow + jnp.sum(dy * r.xc[sl, ln].astype(F32), axis=0, keepdims=True)
                r.rho[:, sl] += head_sums(j, dy * r.y[sl, ln])
                fs = dnn(r.mt[sl, 2 * H : 4 * H], e2)
                if c == 1:
                    k0 = keep_row(j, 0)
                fd = (fs * dy).astype(BF16)
                r.fd[sl, ln] = fd
                ds.append(dnn(ct[c], fd).astype(BF16))
            r.dsb1[:, ln] = ds[1]
            put_state(
                r.ad, j, n, (k0 * ds[1].astype(F32) + ds[0].astype(F32)).astype(BF16)
            )
            r.pk[j, 5:6, :] = grow
            r.pk[j, 6:8, :] = jnp.zeros((2, 128), F32)
            r.skc[...] += head_sums(j, jnp.broadcast_to(srow, (8, 128)))
            return carry

        lax.fori_loop(0, tpc, gates, 0, unroll=2)
        send_pieces(n, r.ad, r.rb2, r.s3, r.r3, cq, me)

    for g in range(NG):
        r.acc[...] = jnp.zeros_like(r.acc)

        def inner(jj, carry, g=g):
            j = g * TPG + jj
            ln = lanes(j)
            for c in range(2):
                sl = blocks[c]
                dyt = r.dy[sl, ln]
                zero = jnp.zeros_like(dyt)
                dybd = jnp.concatenate(
                    [jnp.where(half, dyt, zero), jnp.where(half, zero, dyt)], axis=0
                )
                dw = dnt(dybd, r.xc[sl, ln])
                i = 2 * j + c
                r.acc[0, c] += dw[0:B] * r.lm[i, 0:B, :] + dw[B : 2 * B] * r.lm[i, B : 2 * B, :]
                r.y[sl, ln] = dtn(r.wm[i], dybd)
                sp = row_state(r.ob, j, n, 0) if c == 0 else r.sb1[:, ln]
                r.acc[1, c] += dnt(r.fd[sl, ln], sp)
            return carry

        lax.fori_loop(0, TPG, inner, 0, unroll=2)
        for c in range(2):
            bb, cc = group_parts(g, c)
            dg = r.acc[0, c].astype(BF16)
            r.dbc[blocks[c], g * 128 : (g + 1) * 128] = dtn(dg, cc)
            r.dbc[blocks[c], 256 + g * 128 : 256 + (g + 1) * 128] = r.acc[1, c] + dnn(dg, bb)
        if g == 0:
            owner_scan(n, r.ad, r.rb2, r.pb2, r.ob2, r.kb, r.s3, r.r3, r.s4, r.r4, me, True)
    take_pieces(n, r.pb2, r.ob2, r.s4, r.r4, me)

    r.kap[...] = jnp.zeros_like(r.kap)
    r.tl[...] = jnp.zeros_like(r.tl)
    r.vk[:, :, 0:8, :] = jnp.zeros((2, CONV, 8, 128), F32)
    r.vk[:, :, 8 + T :, :] = jnp.zeros((2, CONV, 8, 128), F32)

    def is_owner(j):
        return (me == j) & (dp == lax.rem(j, ndp))

    def give_tile(j):
        @pl.when(jnp.logical_not(is_owner(j)))
        def _():
            rcopy(
                r.pk.at[j], r.prb.at[mine], r.ps.at[j], r.pr.at[mine],
                {"dp": lax.rem(j, ndp), "ctx": j},
            ).start()

    def conv_back(ext, vk, w, deriv, dxc, j):
        du = dxc.astype(BF16).astype(F32) * deriv
        rows = [jnp.sum(du * ext[8 : 8 + T, :], axis=0, keepdims=True)]
        for k in range(1, CONV):
            v = du * r.live[k - 1]
            rows.append(jnp.sum(v * ext[8 - k : 8 - k + T, :], axis=0, keepdims=True))
            vk[k, 8 : 8 + T, :] = v
        rows.append(jnp.sum(du, axis=0, keepdims=True))
        own = w[0] * du
        prior = jnp.zeros((8, 128), F32)
        for k in range(1, CONV):
            own = own + w[k] * vk[k, 8 + k : 8 + k + T, :]
            prior = prior + w[k] * vk[k, k : k + 8, :]
        r.pk[j, 0 : CONV + 1, :] = jnp.concatenate(rows, axis=0)
        return own, prior

    for g in range(NG):
        r.acc[1] = jnp.zeros((2, B, 128), F32)

        def outer(jj, carry, g=g):
            j = g * TPG + jj
            ln = lanes(j)
            e2 = spread_two(j)
            a1 = row_state(r.ob2, j, n, 0).astype(F32)
            sk = skip_row(j)
            outs = []
            for c in range(2):
                sl = blocks[c]
                if c == 1:
                    ds = a1
                    sp = r.sb1[:, ln]
                else:
                    ds = keep_row(j, 1) * a1 + r.dsb1[:, ln].astype(F32)
                    sp = row_state(r.ob, j, n, 0)
                dsh = ds.astype(BF16)
                xf = r.xc[sl, ln].astype(F32)
                dtte = dnn(r.mt[sl, 0 : 2 * H], e2)
                dxu = dnn(r.bcc[sl, g * 128 : (g + 1) * 128], dsh) * dtte
                r.acc[1, c] += dnt((xf * dtte).astype(BF16), dsh)
                dxs = r.y[sl, ln] + dxu
                ku = jnp.sum(xf * dxu, axis=0, keepdims=True)
                kd = jnp.sum(ds * sp.astype(F32), axis=0, keepdims=True) * keep_row(j, c)
                hs = head_sums(
                    j, jnp.concatenate([xf * dxs, jnp.broadcast_to(ku + kd, (8, 128))], axis=0)
                )
                r.kap[:, sl] += hs[:, 0:B]
                r.tl[:, c * 8 : (c + 1) * 8] += hs[:, B : B + 8]
                outs.append(dxs + sk * r.dy[sl, ln].astype(F32))
            ext = r.ext.at[j % 4]
            ext[8 : 8 + T, :] = r.x[0, :, ln].astype(F32)
            ext[0:8, :] = r.hbuf[8:16, ln].astype(F32)
            own, prior = conv_back(
                ext, r.vk.at[j % 2], x_weights(ln)[0], r.cdx[:, ln],
                jnp.concatenate(outs, axis=0), j,
            )
            r.gx[:, ln] = own.astype(BF16)
            r.tails[:, ln] = own[T - 16 : T]
            r.hb[:, ln] = prior
            give_tile(j)
            return carry

        lax.fori_loop(0, TPG, outer, 0, unroll=2)
        for c in range(2):
            r.dbc[blocks[c], g * 128 : (g + 1) * 128] += r.acc[1, c]

    for j in range(4):
        sl = slice(j * 128, (j + 1) * 128)
        sd = slice(D + j * 128, D + (j + 1) * 128)
        ext = r.ext.at[j]
        ext[8 : 8 + T, :] = r.bc[:, sl].astype(F32)
        ext[0:8, :] = r.hbuf[8:16, sd].astype(F32)
        own, prior = conv_back(
            ext, r.vk.at[j % 2], bc_weights(j)[0], r.cdb[:, sl], r.dbc[:, sl], NT + j
        )
        r.pk[NT + j, 5:8, :] = jnp.zeros((3, 128), F32)
        r.gbc[:, sl] = own.astype(BF16)
        r.tails[:, sd] = own[T - 16 : T]
        r.hb[:, sd] = prior
        give_tile(NT + j)
    back = rcopy(r.hb, r.bbuf, r.sb, r.rb_sem, {"ctx": lax.rem(me + n - 1, n)})

    @pl.when(me > 0)
    def _():
        back.start()

    rev = (iota((B, B), 0) >= iota((B, B), 1)).astype(F32)
    rate_sum = jnp.zeros((H, B), F32)
    bias_sum = jnp.zeros((H, B), F32)
    for c in range(2):
        sl = blocks[c]
        dtv = r.dt[c]
        kp = r.kap[:, sl]
        rr = dnn_full(r.rho[:, sl] - kp, rev) + r.tl[:, c * 8 : c * 8 + 1]
        gd = (kp / dtv - rate * rr) * sigmoid(r.dtr[0, :, sl].astype(F32) + bias)
        r.gdt[:, sl] = gd
        rate_sum = rate_sum - rate * dtv * rr
        bias_sum = bias_sum + gd
    skips = jnp.where(iota((H, B), 1) == 0, r.skc[:, 0:1], 0.0)
    r.pk[nt - 1] = dnt_full(
        ones, jnp.concatenate([rate_sum, bias_sum, skips, jnp.zeros((H, B), F32)], axis=0)
    )
    give_tile(nt - 1)

    @pl.when((me < nt) & (dp == lax.rem(me, ndp)))
    def _():
        r.prb[mine] = r.pk[me]

        def collect(e, total):
            @pl.when(e != mine)
            def _():
                rcopy(
                    r.pk.at[0], r.prb.at[e], r.ps.at[0], r.pr.at[e],
                    {"dp": e // n, "ctx": lax.rem(e, n)},
                ).wait_recv()

            return total + r.prb[e]

        r.pob[me] = lax.fori_loop(0, ne, collect, jnp.zeros((8, 128), F32))

        def give(k, carry):
            e = lax.rem(mine + k, ne)
            rcopy(
                r.pob.at[me], r.pob.at[me], r.as_.at[e], r.ar.at[me],
                {"dp": e // n, "ctx": lax.rem(e, n)},
            ).start()
            return carry

        lax.fori_loop(1, ne, give, 0)

    @pl.when(me < n - 1)
    def _():
        halo.wait_send()
        back.wait_recv()

    @pl.when(me > 0)
    def _():
        back.wait_send()

    def finish(k, carry):
        d = lax.rem(me + k, n)
        to = {"ctx": d}
        rcopy(r.st.at[d], r.rb.at[d], r.s1.at[d], r.r1.at[d], to).wait_send()
        rcopy(r.kr.at[0], r.kb.at[d], r.sk.at[d], r.rk.at[d], to).wait_send()
        rcopy(r.pb.at[d], r.ob.at[d], r.s2.at[d], r.r2.at[d], to).wait_send()
        rcopy(r.ad.at[d], r.rb2.at[d], r.s3.at[d], r.r3.at[d], to).wait_send()
        rcopy(r.pb2.at[d], r.ob2.at[d], r.s4.at[d], r.r4.at[d], to).wait_send()
        return carry

    lax.fori_loop(1, n, finish, 0)

    def tiles_in(j, carry):
        @pl.when(jnp.logical_not(is_owner(j)))
        def _():
            to = {"dp": lax.rem(j, ndp), "ctx": j}
            rcopy(r.pk.at[j], r.prb.at[0], r.ps.at[j], r.pr.at[0], to).wait_send()
            rcopy(r.pob.at[j], r.pob.at[j], r.as_.at[0], r.ar.at[j], to).wait_recv()

        return carry

    lax.fori_loop(0, nt, tiles_in, 0)

    @pl.when((me < nt) & (dp == lax.rem(me, ndp)))
    def _():
        def sent(k, carry):
            e = lax.rem(mine + k, ne)
            rcopy(
                r.pob.at[0], r.pob.at[0], r.as_.at[e], r.ar.at[0],
                {"dp": e // n, "ctx": lax.rem(e, n)},
            ).wait_send()
            return carry

        lax.fori_loop(1, ne, sent, 0)

    r.red[...] = r.pob[...]
    r.rh_o[...] = r.bbuf[...]


def k5_body(scale, red, rh, tail, flg, gx_in, gbc_in,
            gx_o, gbc_o, cw_o, cb_o, bw_o, bb_o, al_o, db_o, sk_o, ga_o):
    f = flg[:, B:T].astype(F32)
    lane = iota((1, B), 1)
    last = jnp.sum(jnp.where(lane == B - 1, f, 0.0))
    two = jnp.sum(jnp.where(lane >= B - 2, f, 0.0))
    row = iota((16, 128), 0)
    keep = jnp.where(row == 15, 1.0, 0.0)
    keep = keep + jnp.where((row == 14) & (last == 0.0), 1.0, 0.0)
    keep = keep + jnp.where((row == 13) & (two == 0.0), 1.0, 0.0)
    for j in range(NT + 4):
        sl = slice(j * 128, (j + 1) * 128)
        add = jnp.concatenate([jnp.zeros((8, 128), F32), rh[:, sl]], axis=0)
        v = (tail[:, sl] + add * keep).astype(BF16)
        t = red[j] * scale
        if j < NT:
            gx_o[:, sl] = v
            cw_o[:, sl] = t[0:4]
            cb_o[:, sl] = t[4:5]
            ga_o[:, sl] = t[5:6]
        else:
            so = slice(j * 128 - D, (j + 1) * 128 - D)
            gbc_o[:, so] = v
            i, sb = (j - NT) // 2, slice(((j - NT) % 2) * 128, ((j - NT) % 2) * 128 + 128)
            for k in range(CONV):
                bw_o[k, i : i + 1, sb] = t[k : k + 1]
            bb_o[i : i + 1, sb] = t[4:5]
    last_tile = red[NT + 4] * scale
    al_o[...] = last_tile[0:1, 0:H]
    db_o[...] = last_tile[0:1, H : 2 * H]
    sk_o[...] = last_tile[0:1, 2 * H : 3 * H]


def sds(*shape, dtype=F32):
    return jax.ShapeDtypeStruct(shape, dtype)


def per_device(
    x_raw, bc_raw, z_gate, dt_raw, resets, conv_x_weight, conv_x_bias, conv_bc_weight,
    conv_bc_bias, a_log, dt_bias, skip_weight, norm_gain, grad_out,
):
    n = lax.axis_size("ctx")
    nh = lax.axis_size("head")
    ndp = lax.axis_size("dp")
    ncq = n // 8
    w = D // ncq
    nt = NT + 5
    ne = n * ndp
    ANY = pl.BlockSpec(memory_space=pl.ANY)
    ins = [
        ("x", x_raw, VM), ("bc", bc_raw[0].reshape(T, DB), VM), ("z_hbm", z_gate, ANY),
        ("go_hbm", grad_out, ANY), ("dtr", dt_raw, VM), ("flg", resets, VM),
        ("alog", a_log.reshape(1, H), VM), ("dtb", dt_bias.reshape(1, H), VM),
        ("cxw", conv_x_weight, VM), ("cxb", conv_x_bias.reshape(1, D), VM),
        ("cbw", conv_bc_weight, VM), ("cbb", conv_bc_bias, VM),
        ("gain", norm_gain.reshape(1, D), VM), ("skip", skip_weight, SM),
    ]
    outs = [
        ("gx", sds(T, D, dtype=BF16)), ("gbc", sds(T, DB, dtype=BF16)),
        ("dz", sds(T, D, dtype=BF16)), ("gdt", sds(H, T)), ("tails", sds(16, D + DB)),
        ("red", sds(nt, 8, 128)), ("rh_o", sds(8, D + DB)),
    ]
    V = pltpu.VMEM
    dma = pltpu.SemaphoreType.DMA
    state = V((n, ROWS, w), BF16)
    scratch = [
        ("z", V((T, D), BF16)), ("go", V((T, D), BF16)), ("zs", dma), ("gs", dma),
        ("ext", V((4, T + 8, 128), F32)), ("cnt", V((T + 8, 128), F32)),
        ("live", V((CONV - 1, T, 128), F32)), ("mask", V((2, B, B), F32)),
        ("dt", V((2, H, B), F32)), ("run", V((2, H, B), F32)), ("mt", V((T, 128), BF16)),
        ("rs", V((T, 128), BF16)), ("tail", V((16, D + DB), BF16)),
        ("hbuf", V((16, D + DB), BF16)), ("xc", V((T, D), BF16)), ("bcc", V((T, DB), BF16)),
        ("cdb", V((T, DB), F32)), ("cdx", V((T, D), F32)), ("fr", V((2, NSTATE, D), F32)),
        ("kr", V((ncq, 1, w), F32)), ("kb", V((n, 1, w), F32)), ("gm", V((B, B), F32)),
        ("lm", V((2 * NT, 2 * B, B), F32)), ("wm", V((2 * NT, 2 * B, B), BF16)),
        ("y", V((T, D), F32)), ("gate", V((T, D), F32)), ("dgate", V((T, D), F32)),
        ("mixed", V((T, D), BF16)), ("sb1", V((NSTATE, D), BF16)),
        ("sums_acc", V((2, T, 128), F32)), ("sums", V((16, T), F32)),
        ("sbuf", V((nh, 16, T), F32)), ("inv", V((T, 128), F32)), ("coef", V((T, 128), F32)),
        ("rho", V((H, T), F32)), ("skc", V((H, 8), F32)), ("dy", V((T, D), BF16)),
        ("fd", V((T, D), BF16)), ("dsb1", V((NSTATE, D), BF16)), ("acc", V((2, 2, B, 128), F32)),
        ("dbc", V((T, DB), F32)), ("kap", V((H, T), F32)), ("tl", V((H, 16), F32)),
        ("vk", V((2, CONV, T + 16, 128), F32)), ("pk", V((nt, 8, 128), F32)),
        ("prb", V((ne, 8, 128), F32)), ("pob", V((nt, 8, 128), F32)),
        ("hb", V((8, D + DB), F32)), ("bbuf", V((8, D + DB), F32)),
        ("st", state), ("rb", state), ("pb", state), ("ob", state),
        ("ad", state), ("rb2", state), ("pb2", state), ("ob2", state),
        ("sh", dma), ("rh", dma), ("sb", dma), ("rb_sem", dma),
        ("hs", dma((nh,))), ("hr", dma((nh,))),
    ]
    scratch += [(k, dma((n,))) for k in ("s1", "r1", "s2", "r2", "s3", "r3", "s4", "r4", "sk", "rk")]
    scratch += [("ps", dma((nt,))), ("ar", dma((nt,))), ("pr", dma((ne,))), ("as_", dma((ne,)))]
    names = [v[0] for v in ins] + [v[0] for v in outs] + [v[0] for v in scratch]
    gx, gbc, dz, gdt, tails, red, rh = pl.pallas_call(
        functools.partial(main_body, n, nh, ndp, nt, names),
        out_shape=[v[1] for v in outs],
        in_specs=[v[2] for v in ins],
        out_specs=[VM] * len(outs),
        scratch_shapes=[v[1] for v in scratch],
        compiler_params=pltpu.CompilerParams(
            vmem_limit_bytes=VLIM, collective_id=0, has_side_effects=True
        ),
    )(*[v[1] for v in ins])
    scale = float(ndp * n * T) ** (-0.5)
    whole = lambda *s: pl.BlockSpec(s, lambda i: (0,) * len(s))
    outs = pl.pallas_call(
        functools.partial(k5_body, scale),
        grid=(1,),
        out_shape=(
            sds(T, D, dtype=BF16), sds(T, DB, dtype=BF16), sds(CONV, D), sds(1, D),
            sds(CONV, 2, DB // 2), sds(2, DB // 2), sds(1, H), sds(1, H), sds(1, H), sds(1, D),
        ),
        in_specs=[
            whole(nt, 8, 128), whole(8, D + DB), whole(16, D + DB), whole(1, T),
            pl.BlockSpec(memory_space=pl.ANY), pl.BlockSpec(memory_space=pl.ANY),
        ],
        out_specs=[
            pl.BlockSpec((16, D), lambda i: (T // 16 - 1, 0)),
            pl.BlockSpec((16, DB), lambda i: (T // 16 - 1, 0)),
            whole(CONV, D), whole(1, D), whole(CONV, 2, DB // 2), whole(2, DB // 2),
            whole(1, H), whole(1, H), whole(1, H), whole(1, D),
        ],
        input_output_aliases={4: 0, 5: 1},
    )(red, rh, tails, resets, gx, gbc)
    gx, gbc, cw, cb, bw, bb, al, db, sk, ga = outs
    return (
        gx[None], gbc.reshape(1, T, 2, DB // 2), dz[None], gdt[None], cw, cb.reshape(D),
        bw, bb, al.reshape(H), db.reshape(H), sk.reshape(H), ga.reshape(D),
    )


def solution(mesh):
    return jax.shard_map(
        per_device,
        mesh=mesh,
        in_specs=(
            P("dp", "ctx", "head"),
            P("dp", "ctx", None, "head"),
            P("dp", "ctx", "head"),
            P("dp", "head", "ctx"),
            P("dp", "ctx"),
            P(None, "head"),
            P("head"),
            P(None, None, "head"),
            P(None, "head"),
            P("head"),
            P("head"),
            P("head"),
            P("head"),
            P("dp", "ctx", "head"),
        ),
        out_specs=(
            P("dp", "ctx", "head"),
            P("dp", "ctx", None, "head"),
            P("dp", "ctx", "head"),
            P("dp", "head", "ctx"),
            P(None, "head"),
            P("head"),
            P(None, None, "head"),
            P(None, "head"),
            P("head"),
            P("head"),
            P("head"),
            P("head"),
        ),
        check_vma=False,
    )
```

time: 1200 us -> 131 us (0.11)
  the two profiles are of different devices: /device:TPU:128 before, /device:TPU:1 now
where the time goes in v2:
time: 131 us
  Pallas kernels  123 us (94%)
  local copies, waits for them, and re-layouts  7.39 us (6%)
    pallas_call x1, Pallas kernels, per_device(): pl.pallas_call(functools.partial(main_body, n, nh, ndp, nt, names), out_s...  121 us
    unnamed x8, local copies, waits for them, and re-layouts  5.67 us

profile of v2, /device:TPU:1, one launch (start us, length us, event | category | flops | bytes accessed | tf_op | source)
XLA Modules:
  0.0 130.9 jit_solution(4907540788880205745)
XLA Ops:
  0.6 1.7 %copy.28 = bf16[32,8,2,256]{3,1,2,0:T(8,128)(2,1)} copy(bf16[32,8,2,256]{3,2,1,0:T(2,128)(2,1)} %bitcast.18) | data formatting | bytes 524288
  2.3 121.1 %shard_map.229 = (bf16[256,2048]{1,0:T(8,128)(2,1)}, bf16[256,512]{1,0:T(8,128)(2,1)}, bf16[256,2048]{1,0:T(8,128)(2,1)}, f32[32,256]{1,0:T(8,128)}, f32[16,2560...) custom-call(bf16[1,256,2048]{2,1,0:T(8,128)(2,1)} %refs_0_.1, bf16[256,512]{1,0:T(8,128)(2,1)} %bitcast.16, ...), custom_call_target="tpu_custom_call" | custom-call | tf_op jit(solution)/shard_map/pallas_call | solution.py:853
  123.4 1.8 %shard_map.230 = (bf16[256,2048]{1,0:T(8,128)(2,1)}, bf16[256,512]{1,0:T(8,128)(2,1)}, f32[4,2048]{1,0:T(4,128)}, f32[1,2048]{1,0:T(1,128)}, f32[4,2,256]{2,1,0:...) custom-call(f32[21,8,128]{2,1,0:T(8,128)} %get-tuple-element.29.red,, ...), custom_call_target="tpu_custom_call", output_to_operand_aliasing={{0}: (4, {}), {1}: (5, {})} | custom-call | tf_op jit(solution)/shard_map/pallas_call | solution.py:865
  125.2 1.7 %reshape.58 = bf16[1,256,2,256]{3,2,1,0:T(2,128)(2,1)} reshape(bf16[256,512]{1,0:T(8,128)(2,1)} %get-tuple-element.35) | data formatting | bytes 524288 | tf_op jit(solution)/shard_map/reshape | solution.py:886
  126.9 0.0 copy-start
  126.9 2.4 %copy.34 = bf16[1,256,2048]{2,1,0:T(8,128)(2,1)} copy(bf16[1,256,2048]{2,1,0:T(8,128)(2,1)} %bitcast.15) | data formatting | bytes 2097152
  129.3 0.0 copy-done
  129.3 0.0 copy-start.1
  129.3 1.0 copy.35
  130.3 0.0 copy-done.1
  130.3 0.6 copy.36
Async XLA Ops:
  126.9 2.4 %copy-start = (bf16[256,2048]{1,0:T(8,128)(2,1)S(1)}, bf16[256,2048]{1,0:T(8,128)(2,1)}, u32[]{:S(2)}) copy-start(bf16[256,2048]{1,0:T(8,128)(2,1)} %get-tuple-element.36) | copy-start | bytes 3145732
  129.3 1.0 copy-start.1

commit v3 on v2

--- a/solution.py
+++ b/solution.py
@@ -164,7 +164,7 @@
 
         @pl.when(to != me)
         def _():
-            rcopy(st.at[to], rb.at[me], s1.at[to], r1.at[me], {"ctx": to}).start()
+            rcopy(st.at[to], rb.at[me], s1, r1, {"ctx": to}).start()
 
         return carry
 
@@ -173,19 +173,17 @@
 
 def owner_scan(n, st, rb, pb, ob, kb, s1, r1, s2, r2, me, backward):
     rb[me] = st[me]
+    others = pl.ds(0, n - 1)
+    rcopy(st.at[others], rb.at[others], s1, r1, {"ctx": me}).wait_recv()
 
     def step(i, acc):
         d = n - 1 - i if backward else i
 
+        pb[d] = acc.astype(BF16)
+
         @pl.when(d != me)
         def _():
-            rcopy(st.at[0], rb.at[d], s1.at[d], r1.at[d], {"ctx": d}).wait_recv()
-
-        pb[d] = acc.astype(BF16)
-
-        @pl.when(d != me)
-        def _():
-            rcopy(pb.at[d], ob.at[me], s2.at[d], r2.at[me], {"ctx": d}).start()
+            rcopy(pb.at[d], ob.at[me], s2, r2, {"ctx": d}).start()
 
         return kb[d] * acc + rb[d].astype(F32)
 
@@ -194,12 +192,8 @@
 
 
 def take_pieces(n, pb, ob, s2, r2, me):
-    def step(k, carry):
-        d = lax.rem(me + k, n)
-        rcopy(pb.at[d], ob.at[d], s2.at[d], r2.at[d], {"ctx": d}).wait_recv()
-        return carry
-
-    lax.fori_loop(1, n, step, 0)
+    others = pl.ds(0, n - 1)
+    rcopy(pb.at[others], ob.at[others], s2, r2, {"ctx": me}).wait_recv()
 
 
 def main_body(n, nh, ndp, nt, names, *refs):
@@ -327,7 +321,7 @@
             r.fr[1, :, lanes(j)] = dnn(bt, x_conv(j, 1))
             return carry
 
-        lax.fori_loop(0, TPG, second, 0, unroll=2)
+        lax.fori_loop(0, TPG, second, 0, unroll=4)
         if g == 0:
             pl.semaphore_wait(barrier, ne - 1 + nh - 1)
             halo = rcopy(r.tail, r.hbuf, r.sh, r.rh, {"ctx": lax.rem(me + 1, n)})
@@ -355,7 +349,7 @@
             r.kr[cq, :, lanes(jj)] = keep_row(j, 0) * k1
             return carry
 
-        lax.fori_loop(0, tpc, first, 0, unroll=2)
+        lax.fori_loop(0, tpc, first, 0, unroll=4)
         send_pieces(n, r.st, r.rb, r.s1, r.r1, cq, me)
 
         def send_row(rz, carry, cq=cq):
@@ -363,7 +357,7 @@
 
             @pl.when(to != me)
             def _():
-                rcopy(r.kr.at[cq], r.kb.at[me], r.sk.at[to], r.rk.at[me], {"ctx": to}).start()
+                rcopy(r.kr.at[cq], r.kb.at[me], r.sk, r.rk, {"ctx": to}).start()
 
             return carry
 
@@ -402,16 +396,12 @@
                 r.y[blocks[c], ln] = dnn(jnp.concatenate(ws, axis=1), xbd)
                 return carry
 
-            lax.fori_loop(0, TPG, inside, 0, unroll=2)
+            lax.fori_loop(0, TPG, inside, 0, unroll=4)
 
     r.kb[me] = r.kr[lax.rem(me, ncq)]
 
-    def rows_in(k, carry):
-        d = lax.rem(me + k, n)
-        rcopy(r.kr.at[0], r.kb.at[d], r.sk.at[d], r.rk.at[d], {"ctx": d}).wait_recv()
-        return carry
-
-    lax.fori_loop(1, n, rows_in, 0)
+    others = pl.ds(0, n - 1)
+    rcopy(r.kb.at[others], r.kb.at[others], r.sk, r.rk, {"ctx": me}).wait_recv()
     owner_scan(n, r.st, r.rb, r.pb, r.ob, r.kb, r.s1, r.r1, r.s2, r.r2, me, False)
 
     zcopy.wait()
@@ -432,7 +422,7 @@
             r.cdx[blocks[c], ln] = sg * (1.0 + u * (1.0 - sg))
         return carry
 
-    lax.fori_loop(0, NT, prepare, 0)
+    lax.fori_loop(0, NT, prepare, 0, unroll=2)
     take_pieces(n, r.pb, r.ob, r.s2, r.r2, me)
 
     r.sums_acc[...] = jnp.zeros_like(r.sums_acc)
@@ -462,7 +452,7 @@
                 r.sums_acc[1, sl, :] += gated * gained
             return carry
 
-        lax.fori_loop(0, TPG, outputs, 0, unroll=2)
+        lax.fori_loop(0, TPG, outputs, 0, unroll=4)
     ones = jnp.ones((8, 128), F32)
     r.sums[0:8, :] = dnt_full(ones, r.sums_acc[0])
     r.sums[8:16, :] = dnt_full(ones, r.sums_acc[1])
@@ -530,7 +520,7 @@
             r.skc[...] += head_sums(j, jnp.broadcast_to(srow, (8, 128)))
             return carry
 
-        lax.fori_loop(0, tpc, gates, 0, unroll=2)
+        lax.fori_loop(0, tpc, gates, 0, unroll=4)
         send_pieces(n, r.ad, r.rb2, r.s3, r.r3, cq, me)
 
     for g in range(NG):
@@ -554,7 +544,7 @@
                 r.acc[1, c] += dnt(r.fd[sl, ln], sp)
             return carry
 
-        lax.fori_loop(0, TPG, inner, 0, unroll=2)
+        lax.fori_loop(0, TPG, inner, 0, unroll=4)
         for c in range(2):
             bb, cc = group_parts(g, c)
             dg = r.acc[0, c].astype(BF16)
@@ -576,7 +566,7 @@
         @pl.when(jnp.logical_not(is_owner(j)))
         def _():
             rcopy(
-                r.pk.at[j], r.prb.at[mine], r.ps.at[j], r.pr.at[mine],
+                r.pk.at[j], r.prb.at[mine], r.ps, r.pr,
                 {"dp": lax.rem(j, ndp), "ctx": j},
             ).start()
 
@@ -687,22 +677,18 @@
     def _():
         r.prb[mine] = r.pk[me]
 
+        alls = pl.ds(0, ne - 1)
+        rcopy(r.prb.at[alls], r.prb.at[alls], r.ps, r.pr, {"ctx": me}).wait_recv()
+
         def collect(e, total):
-            @pl.when(e != mine)
-            def _():
-                rcopy(
-                    r.pk.at[0], r.prb.at[e], r.ps.at[0], r.pr.at[e],
-                    {"dp": e // n, "ctx": lax.rem(e, n)},
-                ).wait_recv()
-
             return total + r.prb[e]
 
-        r.pob[me] = lax.fori_loop(0, ne, collect, jnp.zeros((8, 128), F32))
+        r.pob[me] = lax.fori_loop(0, ne, collect, jnp.zeros((8, 128), F32), unroll=8)
 
         def give(k, carry):
             e = lax.rem(mine + k, ne)
             rcopy(
-                r.pob.at[me], r.pob.at[me], r.as_.at[e], r.ar.at[me],
+                r.pob.at[me], r.pob.at[me], r.as_, r.ar,
                 {"dp": e // n, "ctx": lax.rem(e, n)},
             ).start()
             return carry
@@ -718,40 +704,22 @@
     def _():
         back.wait_send()
 
-    def finish(k, carry):
-        d = lax.rem(me + k, n)
-        to = {"ctx": d}
-        rcopy(r.st.at[d], r.rb.at[d], r.s1.at[d], r.r1.at[d], to).wait_send()
-        rcopy(r.kr.at[0], r.kb.at[d], r.sk.at[d], r.rk.at[d], to).wait_send()
-        rcopy(r.pb.at[d], r.ob.at[d], r.s2.at[d], r.r2.at[d], to).wait_send()
-        rcopy(r.ad.at[d], r.rb2.at[d], r.s3.at[d], r.r3.at[d], to).wait_send()
-        rcopy(r.pb2.at[d], r.ob2.at[d], r.s4.at[d], r.r4.at[d], to).wait_send()
-        return carry
-
-    lax.fori_loop(1, n, finish, 0)
-
-    def tiles_in(j, carry):
-        @pl.when(jnp.logical_not(is_owner(j)))
-        def _():
-            to = {"dp": lax.rem(j, ndp), "ctx": j}
-            rcopy(r.pk.at[j], r.prb.at[0], r.ps.at[j], r.pr.at[0], to).wait_send()
-            rcopy(r.pob.at[j], r.pob.at[j], r.as_.at[0], r.ar.at[j], to).wait_recv()
-
-        return carry
-
-    lax.fori_loop(0, nt, tiles_in, 0)
-
-    @pl.when((me < nt) & (dp == lax.rem(me, ndp)))
+    rcopy(r.kb.at[others], r.kb.at[others], r.sk, r.rk, {"ctx": me}).wait_send()
+    for sent in (r.s1, r.s2, r.s3, r.s4):
+        rcopy(r.st.at[others], r.rb.at[others], sent, sent, {"ctx": me}).wait_send()
+
+    owns = (me < nt) & (dp == lax.rem(me, ndp))
+
+    @pl.when(owns)
     def _():
-        def sent(k, carry):
-            e = lax.rem(mine + k, ne)
-            rcopy(
-                r.pob.at[0], r.pob.at[0], r.as_.at[e], r.ar.at[0],
-                {"dp": e // n, "ctx": lax.rem(e, n)},
-            ).wait_send()
-            return carry
-
-        lax.fori_loop(1, ne, sent, 0)
+        alls = pl.ds(0, ne - 1)
+        most = pl.ds(0, nt - 1)
+        rcopy(r.prb.at[alls], r.prb.at[alls], r.as_, r.ar, {"ctx": me}).wait_send()
+        rcopy(r.pk.at[most], r.pob.at[most], r.ps, r.ar, {"ctx": me}).wait()
+
+    @pl.when(jnp.logical_not(owns))
+    def _():
+        rcopy(r.pk, r.pob, r.ps, r.ar, {"ctx": me}).wait()
 
     r.red[...] = r.pob[...]
     r.rh_o[...] = r.bbuf[...]
@@ -847,8 +815,12 @@
         ("sh", dma), ("rh", dma), ("sb", dma), ("rb_sem", dma),
         ("hs", dma((nh,))), ("hr", dma((nh,))),
     ]
-    scratch += [(k, dma((n,))) for k in ("s1", "r1", "s2", "r2", "s3", "r3", "s4", "r4", "sk", "rk")]
-    scratch += [("ps", dma((nt,))), ("ar", dma((nt,))), ("pr", dma((ne,))), ("as_", dma((ne,)))]
+    scratch += [
+        (k, dma)
+        for k in (
+            "s1", "r1", "s2", "r2", "s3", "r3", "s4", "r4", "sk", "rk", "ps", "ar", "pr", "as_"
+        )
+    ]
     names = [v[0] for v in ins] + [v[0] for v in outs] + [v[0] for v in scratch]
     gx, gbc, dz, gdt, tails, red, rh = pl.pallas_call(
         functools.partial(main_body, n, nh, ndp, nt, names),

time: 131 us -> 126 us (0.962)
  Pallas kernels: 123 us -> 118 us
    pallas_call x1, Pallas kernels: 121 us -> 116 us  [per_device(): pl.pallas_call(functools.partial(main_body, n, nh, ndp, nt, names), out_s...]
where the time goes in v3:
time: 126 us
  Pallas kernels  118 us (94%)
  local copies, waits for them, and re-layouts  7.39 us (6%)
    pallas_call x1, Pallas kernels, per_device(): pl.pallas_call(functools.partial(main_body, n, nh, ndp, nt, names), out_s...  116 us
    unnamed x8, local copies, waits for them, and re-layouts  5.67 us

profile of v3, /device:TPU:1, one launch (start us, length us, event | category | flops | bytes accessed | tf_op | source)
XLA Modules:
  0.0 125.7 jit_solution(830218979681112583)
XLA Ops:
  0.6 1.7 %copy.28 = bf16[32,8,2,256]{3,1,2,0:T(8,128)(2,1)} copy(bf16[32,8,2,256]{3,2,1,0:T(2,128)(2,1)} %bitcast.18) | data formatting | bytes 524288
  2.3 115.8 %shard_map.229 = (bf16[256,2048]{1,0:T(8,128)(2,1)}, bf16[256,512]{1,0:T(8,128)(2,1)}, bf16[256,2048]{1,0:T(8,128)(2,1)}, f32[32,256]{1,0:T(8,128)}, f32[16,2560...) custom-call(bf16[1,256,2048]{2,1,0:T(8,128)(2,1)} %refs_0_.1, bf16[256,512]{1,0:T(8,128)(2,1)} %bitcast.16, ...), custom_call_target="tpu_custom_call" | custom-call | tf_op jit(solution)/shard_map/pallas_call | solution.py:825
  118.2 1.8 %shard_map.230 = (bf16[256,2048]{1,0:T(8,128)(2,1)}, bf16[256,512]{1,0:T(8,128)(2,1)}, f32[4,2048]{1,0:T(4,128)}, f32[1,2048]{1,0:T(1,128)}, f32[4,2,256]{2,1,0:...) custom-call(f32[21,8,128]{2,1,0:T(8,128)} %get-tuple-element.29.red,, ...), custom_call_target="tpu_custom_call", output_to_operand_aliasing={{0}: (4, {}), {1}: (5, {})} | custom-call | tf_op jit(solution)/shard_map/pallas_call | solution.py:837
  119.9 1.7 %reshape.58 = bf16[1,256,2,256]{3,2,1,0:T(2,128)(2,1)} reshape(bf16[256,512]{1,0:T(8,128)(2,1)} %get-tuple-element.35) | data formatting | bytes 524288 | tf_op jit(solution)/shard_map/reshape | solution.py:858
  121.7 0.0 copy-start
  121.7 2.4 %copy.34 = bf16[1,256,2048]{2,1,0:T(8,128)(2,1)} copy(bf16[1,256,2048]{2,1,0:T(8,128)(2,1)} %bitcast.15) | data formatting | bytes 2097152
  124.1 0.0 copy-done
  124.1 0.0 copy-start.1
  124.1 1.0 copy.35
  125.0 0.0 copy-done.1
  125.0 0.6 copy.36
Async XLA Ops:
  121.7 2.4 %copy-start = (bf16[256,2048]{1,0:T(8,128)(2,1)S(1)}, bf16[256,2048]{1,0:T(8,128)(2,1)}, u32[]{:S(2)}) copy-start(bf16[256,2048]{1,0:T(8,128)(2,1)} %get-tuple-element.36) | copy-start | bytes 3145732
  124.1 1.0 copy-start.1

commit v4 on v3

--- a/solution.py
+++ b/solution.py
@@ -93,19 +93,6 @@
     return ((row % H == 2 * j + lane // 128) & (row < 3 * H)).astype(BF16)
 
 
-def collect_two(j):
-    row = iota((H, 128), 0)
-    lane = iota((H, 128), 1)
-    return (row == 2 * j + lane // HEAD_DIM).astype(BF16)
-
-
-def head_sums(j, v):
-    high = v.astype(BF16)
-    low = (v - high.astype(F32)).astype(BF16)
-    e = collect_two(j)
-    return dnt(e, high) + dnt(e, low)
-
-
 def conv_input(ext, live, w, bias, lo, rows):
     u = bias + w[0] * ext[8 + lo : 8 + lo + rows, :]
     for k in range(1, CONV):
@@ -119,28 +106,29 @@
         live[k - 1] = (now == cnt[8 - k : 8 - k + T, :]).astype(F32)
 
 
-def block_mask(rt, q, c):
-    qc = rt[c * B : (c + 1) * B, H : H + 1]
-    qr = q[0:1, c * B : (c + 1) * B]
-    ok = (qc == qr) & (iota((B, B), 0) >= iota((B, B), 1))
-    return jnp.where(ok, 0.0, -1e30)
-
-
-def row_state(ref, j, n, lead):
+def row_state(ref, jj, n):
     ncq = n // 8
-    tpc = NT // ncq
-    cq = j // tpc
-    lane = lanes(j % tpc)
+    tpc = TPG // ncq
+    cq = jj // tpc
+    lane = lanes(jj % tpc)
     return jnp.concatenate([ref[rz * ncq + cq, :, lane] for rz in range(8)], axis=0)
 
 
-def put_state(ref, j, n, v):
+def put_state(ref, jj, n, v):
     ncq = n // 8
-    tpc = NT // ncq
-    cq = j // tpc
-    lane = lanes(j % tpc)
+    tpc = TPG // ncq
+    cq = jj // tpc
+    lane = lanes(jj % tpc)
     for rz in range(8):
         ref[rz * ncq + cq, :, lane] = v[rz * ROWS : (rz + 1) * ROWS]
+
+
+def head_rows(v):
+    t = v.T
+    return (
+        jnp.sum(t[0:HEAD_DIM], axis=0, keepdims=True),
+        jnp.sum(t[HEAD_DIM:], axis=0, keepdims=True),
+    )
 
 
 def column(row):
@@ -156,7 +144,7 @@
     )
 
 
-def send_pieces(n, st, rb, s1, r1, cq, me):
+def send_pieces(n, cq, me, st, rb, pb, ob, s1, r1, s2, r2):
     ncq = n // 8
 
     def send(rz, carry):
@@ -171,7 +159,7 @@
     lax.fori_loop(0, 8, send, 0)
 
 
-def owner_scan(n, st, rb, pb, ob, kb, s1, r1, s2, r2, me, backward):
+def owner_scan(n, half, kb, st, rb, pb, ob, s1, r1, s2, r2, me, backward):
     rb[me] = st[me]
     others = pl.ds(0, n - 1)
     rcopy(st.at[others], rb.at[others], s1, r1, {"ctx": me}).wait_recv()
@@ -185,13 +173,13 @@
         def _():
             rcopy(pb.at[d], ob.at[me], s2, r2, {"ctx": d}).start()
 
-        return kb[d] * acc + rb[d].astype(F32)
+        return kb[d, :, half] * acc + rb[d].astype(F32)
 
     lax.fori_loop(0, n, step, jnp.zeros(rb.shape[1:], F32))
     ob[me] = pb[me]
 
 
-def take_pieces(n, pb, ob, s2, r2, me):
+def take_pieces(n, me, st, rb, pb, ob, s1, r1, s2, r2):
     others = pl.ds(0, n - 1)
     rcopy(pb.at[others], ob.at[others], s2, r2, {"ctx": me}).wait_recv()
 
@@ -199,7 +187,7 @@
 def main_body(n, nh, ndp, nt, names, *refs):
     r = types.SimpleNamespace(**dict(zip(names, refs)))
     ncq = n // 8
-    tpc = NT // ncq
+    wh = TPG * 128 // ncq
     me = lax.axis_index("ctx")
     dp = lax.axis_index("dp")
     hd = lax.axis_index("head")
@@ -208,6 +196,12 @@
     half = iota((B, 128), 1) < HEAD_DIM
     lane1 = iota((1, 128), 1)
     blocks = [slice(0, B), slice(B, T)]
+    halves = [slice(g * wh, (g + 1) * wh) for g in range(NG)]
+    parts = ("st", "rb", "pb", "ob", "s1", "r1", "s2", "r2")
+    fwd = [[getattr(r, k + "f" + str(g)) for k in parts] for g in range(NG)]
+    bwd = [[getattr(r, k + "b" + str(g)) for k in parts] for g in range(NG)]
+    states = [f[3] for f in fwd]
+    laters = [f[3] for f in bwd]
 
     r.hbuf[...] = jnp.zeros_like(r.hbuf)
     r.bbuf[...] = jnp.zeros_like(r.bbuf)
@@ -229,6 +223,8 @@
     gcopy = pltpu.make_async_copy(r.go_hbm.at[0], r.go, r.gs)
     zcopy.start()
     gcopy.start()
+    r.bc[...] = r.bc_raw[0].reshape(T, DB)
+    r.hsr[...] = jnp.zeros_like(r.hsr)
 
     rate = jnp.exp(column(r.alog[...]))
     bias = column(r.dtb[...])
@@ -263,6 +259,20 @@
         r.mask[c] = jnp.where(ok, 0.0, -1e30)
     live_masks(r.cnt, r.live)
 
+    def keeps(j, carry):
+        e2 = spread_two(j)
+        k0, k1 = [
+            dnn(r.mt[(c + 1) * B - 16 : (c + 1) * B, 2 * H : 4 * H], e2)[15:16] for c in range(2)
+        ]
+        r.krow[0, :, lanes(j)] = k0
+        r.krow[1, :, lanes(j)] = k1
+        tpc = TPG // ncq
+        jj = j % TPG
+        r.kr[jj // tpc, :, lanes((j // TPG) * tpc + jj % tpc)] = k0 * k1
+        return carry
+
+    lax.fori_loop(0, NT, keeps, 0, unroll=4)
+
     row16 = iota((16, 128), 0)
     same = (r.cnt[8 + T - 16 : 8 + T, :] == r.cnt[8 + T - 1 : 8 + T, :])
     for j in range(NT + 4):
@@ -304,13 +314,12 @@
         xc = (u * sigmoid(u)).astype(BF16)
         r.xc[blocks[c], ln] = xc
         dtte = dnn(r.mt[blocks[c], 0 : 2 * H], spread_two(j))
-        return (xc.astype(F32) * dtte).astype(BF16)
+        uu = (xc.astype(F32) * dtte).astype(BF16)
+        r.uu[blocks[c], ln] = uu
+        return uu
 
     def b_turned(g, c):
         return r.bcc[blocks[c], g * 128 : (g + 1) * 128].astype(F32).T.astype(BF16)
-
-    def keep_row(j, c):
-        return dnn(r.mt[(c + 1) * B - 16 : (c + 1) * B, 2 * H : 4 * H], spread_two(j))[15:16]
 
     bc_conv(1)
     for g in range(NG):
@@ -330,38 +339,38 @@
             def _():
                 halo.start()
 
+            def send_row(k, carry):
+                to = lax.rem(me + k, n)
+                rcopy(
+                    r.kr.at[lax.rem(to, ncq)], r.kb.at[me], r.sk, r.rk, {"ctx": to}
+                ).start()
+                return carry
+
+            lax.fori_loop(1, n, send_row, 0)
+
     @pl.when(me > 0)
     def _():
         halo.wait_recv()
 
     bc_conv(0)
-    bts = [b_turned(g, 0) for g in range(NG)]
-    for cq in range(ncq):
-        bt = bts[cq * tpc // TPG]
-
-        def first(jj, carry, cq=cq, bt=bt):
-            j = cq * tpc + jj
-            ln = lanes(j)
-            fresh = dnn(bt, x_conv(j, 0))
-            r.fr[0, :, ln] = fresh
-            k1 = keep_row(j, 1)
-            put_state(r.st, j, n, (k1 * fresh + r.fr[1, :, ln]).astype(BF16))
-            r.kr[cq, :, lanes(jj)] = keep_row(j, 0) * k1
-            return carry
-
-        lax.fori_loop(0, tpc, first, 0, unroll=4)
-        send_pieces(n, r.st, r.rb, r.s1, r.r1, cq, me)
-
-        def send_row(rz, carry, cq=cq):
-            to = rz * ncq + cq
-
-            @pl.when(to != me)
-            def _():
-                rcopy(r.kr.at[cq], r.kb.at[me], r.sk, r.rk, {"ctx": to}).start()
-
-            return carry
-
-        lax.fori_loop(0, 8, send_row, 0)
+    for g in range(NG):
+        bt = b_turned(g, 0)
+        for hf in range(2):
+
+            def first(i, carry, g=g, hf=hf, bt=bt):
+                jj = hf * 4 + i
+                j = g * TPG + jj
+                ln = lanes(j)
+                fresh = dnn(bt, x_conv(j, 0))
+                r.fr[0, :, ln] = fresh
+                put_state(
+                    fwd[g][0], jj, n, (r.krow[1, :, ln] * fresh + r.fr[1, :, ln]).astype(BF16)
+                )
+                return carry
+
+            lax.fori_loop(0, 4, first, 0, unroll=4)
+            for cq in range(hf * ncq // 2, (hf + 1) * ncq // 2):
+                send_pieces(n, cq, me, *fwd[g])
 
     def group_parts(g, c):
         return (
@@ -402,7 +411,7 @@
 
     others = pl.ds(0, n - 1)
     rcopy(r.kb.at[others], r.kb.at[others], r.sk, r.rk, {"ctx": me}).wait_recv()
-    owner_scan(n, r.st, r.rb, r.pb, r.ob, r.kb, r.s1, r.r1, r.s2, r.r2, me, False)
+    owner_scan(n, halves[0], r.kb, *fwd[0], me, False)
 
     zcopy.wait()
     gcopy.wait()
@@ -422,8 +431,9 @@
             r.cdx[blocks[c], ln] = sg * (1.0 + u * (1.0 - sg))
         return carry
 
-    lax.fori_loop(0, NT, prepare, 0, unroll=2)
-    take_pieces(n, r.pb, r.ob, r.s2, r.r2, me)
+    lax.fori_loop(0, TPG, prepare, 0, unroll=2)
+    owner_scan(n, halves[1], r.kb, *fwd[1], me, False)
+    lax.fori_loop(TPG, NT, prepare, 0, unroll=2)
 
     r.sums_acc[...] = jnp.zeros_like(r.sums_acc)
 
@@ -432,13 +442,14 @@
 
     for g in range(NG):
         ccs = [group_parts(g, c)[1] for c in range(2)]
+        take_pieces(n, me, *fwd[g])
 
         def outputs(jj, carry, g=g, ccs=ccs):
             j = g * TPG + jj
             ln = lanes(j)
             fs = dnn(r.mt[:, 2 * H : 4 * H], spread_two(j))
-            sb0 = row_state(r.ob, j, n, 0)
-            sb1 = (fs[B - 1 : B] * sb0.astype(F32) + r.fr[0, :, ln]).astype(BF16)
+            sb0 = row_state(states[g], jj, n)
+            sb1 = (r.krow[0, :, ln] * sb0.astype(F32) + r.fr[0, :, ln]).astype(BF16)
             r.sb1[:, ln] = sb1
             for c in range(2):
                 sl = blocks[c]
@@ -464,11 +475,11 @@
         copies[-1].start()
     for cp in copies:
         cp.wait()
-    parts = [r.sums[...]] + [r.sbuf[k] for k in range(1, nh)]
-    total = jnp.zeros_like(parts[0])
+    shares = [r.sums[...]] + [r.sbuf[k] for k in range(1, nh)]
+    total = jnp.zeros_like(shares[0])
     for d in range(nh):
         for k in range(nh):
-            total = total + jnp.where(lax.rem(hd - k + nh, nh) == d, parts[k], 0.0)
+            total = total + jnp.where(lax.rem(hd - k + nh, nh) == d, shares[k], 0.0)
     inv = lax.rsqrt(total[0:8] / INNER + EPS)
     coef = inv * inv * inv * total[8:16] / INNER
     for c in range(2):
@@ -477,51 +488,52 @@
         r.inv[sl, :] = jnp.broadcast_to(tr[:, 0:1], (B, 128))
         r.coef[sl, :] = jnp.broadcast_to(tr[:, 8:9], (B, 128))
 
-    r.rho[...] = jnp.zeros_like(r.rho)
-    r.skc[...] = jnp.zeros_like(r.skc)
-    cts = [[group_parts(g, c)[1].astype(F32).T.astype(BF16) for c in range(2)] for g in range(NG)]
-    for cq in range(ncq):
-        ct = cts[cq * tpc // TPG]
-
-        def gates(jj, carry, cq=cq, ct=ct):
-            j = cq * tpc + jj
-            ln = lanes(j)
-            e2 = spread_two(j)
-            grow = jnp.zeros((1, 128), F32)
-            srow = jnp.zeros((1, 128), F32)
-            ds = []
-            for c in range(2):
-                sl = blocks[c]
-                m = r.mixed[sl, ln].astype(F32)
-                gt = r.gate[sl, ln]
-                go = r.go[sl, ln].astype(F32)
-                gated = m * gt
-                iv = r.inv[sl, :]
-                dg = go * r.gain[0:1, ln] * iv - gated * r.coef[sl, :]
-                grow = grow + jnp.sum(go * gated * iv, axis=0, keepdims=True)
-                r.dz[sl, ln] = (dg * m * r.dgate[sl, ln]).astype(BF16)
-                dm = (dg * gt).astype(BF16)
-                r.dy[sl, ln] = dm
-                dy = dm.astype(F32)
-                srow = srow + jnp.sum(dy * r.xc[sl, ln].astype(F32), axis=0, keepdims=True)
-                r.rho[:, sl] += head_sums(j, dy * r.y[sl, ln])
-                fs = dnn(r.mt[sl, 2 * H : 4 * H], e2)
-                if c == 1:
-                    k0 = keep_row(j, 0)
-                fd = (fs * dy).astype(BF16)
-                r.fd[sl, ln] = fd
-                ds.append(dnn(ct[c], fd).astype(BF16))
-            r.dsb1[:, ln] = ds[1]
-            put_state(
-                r.ad, j, n, (k0 * ds[1].astype(F32) + ds[0].astype(F32)).astype(BF16)
-            )
-            r.pk[j, 5:6, :] = grow
-            r.pk[j, 6:8, :] = jnp.zeros((2, 128), F32)
-            r.skc[...] += head_sums(j, jnp.broadcast_to(srow, (8, 128)))
-            return carry
-
-        lax.fori_loop(0, tpc, gates, 0, unroll=4)
-        send_pieces(n, r.ad, r.rb2, r.s3, r.r3, cq, me)
+    for g in range(NG):
+        ct = [group_parts(g, c)[1].astype(F32).T.astype(BF16) for c in range(2)]
+        for hf in range(2):
+
+            def gates(i, carry, g=g, hf=hf, ct=ct):
+                jj = hf * 4 + i
+                j = g * TPG + jj
+                ln = lanes(j)
+                e2 = spread_two(j)
+                grow = jnp.zeros((1, 128), F32)
+                srow = jnp.zeros((1, 128), F32)
+                ds = []
+                for c in range(2):
+                    sl = blocks[c]
+                    m = r.mixed[sl, ln].astype(F32)
+                    gt = r.gate[sl, ln]
+                    gated = m * gt
+                    gi = r.go[sl, ln].astype(F32) * r.inv[sl, :]
+                    dg = gi * r.gain[0:1, ln] - gated * r.coef[sl, :]
+                    grow = grow + jnp.sum(gi * gated, axis=0, keepdims=True)
+                    r.dzv[sl, ln] = (dg * m * r.dgate[sl, ln]).astype(BF16)
+                    dm = (dg * gt).astype(BF16)
+                    r.dy[sl, ln] = dm
+                    dy = dm.astype(F32)
+                    srow = srow + jnp.sum(dy * r.xc[sl, ln].astype(F32), axis=0, keepdims=True)
+                    h0, h1 = head_rows(dy * r.y[sl, ln])
+                    r.rho[c, pl.ds(2 * j, 1), :] = h0
+                    r.rho[c, pl.ds(2 * j + 1, 1), :] = h1
+                    fd = (dnn(r.mt[sl, 2 * H : 4 * H], e2) * dy).astype(BF16)
+                    r.fd[sl, ln] = fd
+                    ds.append(dnn(ct[c], fd).astype(BF16))
+                r.dsb1[:, ln] = ds[1]
+                put_state(
+                    bwd[g][0], jj, n,
+                    (r.krow[0, :, ln] * ds[1].astype(F32) + ds[0].astype(F32)).astype(BF16),
+                )
+                r.pk[j, 5:6, :] = grow
+                r.pk[j, 6:8, :] = jnp.zeros((2, 128), F32)
+                r.hsr[2:3, ln] = srow
+                return carry
+
+            lax.fori_loop(0, 4, gates, 0, unroll=4)
+            for cq in range(hf * ncq // 2, (hf + 1) * ncq // 2):
+                send_pieces(n, cq, me, *bwd[g])
+    zout = pltpu.make_async_copy(r.dzv, r.dz, r.zo)
+    zout.start()
 
     for g in range(NG):
         r.acc[...] = jnp.zeros_like(r.acc)
@@ -540,7 +552,7 @@
                 i = 2 * j + c
                 r.acc[0, c] += dw[0:B] * r.lm[i, 0:B, :] + dw[B : 2 * B] * r.lm[i, B : 2 * B, :]
                 r.y[sl, ln] = dtn(r.wm[i], dybd)
-                sp = row_state(r.ob, j, n, 0) if c == 0 else r.sb1[:, ln]
+                sp = row_state(states[g], jj, n) if c == 0 else r.sb1[:, ln]
                 r.acc[1, c] += dnt(r.fd[sl, ln], sp)
             return carry
 
@@ -550,12 +562,8 @@
             dg = r.acc[0, c].astype(BF16)
             r.dbc[blocks[c], g * 128 : (g + 1) * 128] = dtn(dg, cc)
             r.dbc[blocks[c], 256 + g * 128 : 256 + (g + 1) * 128] = r.acc[1, c] + dnn(dg, bb)
-        if g == 0:
-            owner_scan(n, r.ad, r.rb2, r.pb2, r.ob2, r.kb, r.s3, r.r3, r.s4, r.r4, me, True)
-    take_pieces(n, r.pb2, r.ob2, r.s4, r.r4, me)
-
-    r.kap[...] = jnp.zeros_like(r.kap)
-    r.tl[...] = jnp.zeros_like(r.tl)
+        owner_scan(n, halves[g], r.kb, *bwd[g], me, True)
+
     r.vk[:, :, 0:8, :] = jnp.zeros((2, CONV, 8, 128), F32)
     r.vk[:, :, 8 + T :, :] = jnp.zeros((2, CONV, 8, 128), F32)
 
@@ -570,68 +578,85 @@
                 {"dp": lax.rem(j, ndp), "ctx": j},
             ).start()
 
-    def conv_back(ext, vk, w, deriv, dxc, j):
-        du = dxc.astype(BF16).astype(F32) * deriv
-        rows = [jnp.sum(du * ext[8 : 8 + T, :], axis=0, keepdims=True)]
+    def conv_back(c, ext, vk, w, deriv, dxc, rows):
+        sl = blocks[c]
+        lo = c * B
+        du = dxc * deriv
+        rows[0] = rows[0] + jnp.sum(du * ext[8 + lo : 8 + lo + B, :], axis=0, keepdims=True)
+        rows[CONV] = rows[CONV] + jnp.sum(du, axis=0, keepdims=True)
+        own = w[0] * du
         for k in range(1, CONV):
-            v = du * r.live[k - 1]
-            rows.append(jnp.sum(v * ext[8 - k : 8 - k + T, :], axis=0, keepdims=True))
-            vk[k, 8 : 8 + T, :] = v
-        rows.append(jnp.sum(du, axis=0, keepdims=True))
-        own = w[0] * du
+            v = du * r.live[k - 1, sl, :]
+            rows[k] = rows[k] + jnp.sum(
+                v * ext[8 - k + lo : 8 - k + lo + B, :], axis=0, keepdims=True
+            )
+            vk[k, 8 + lo : 8 + lo + B, :] = v
+        for k in range(1, CONV):
+            own = own + w[k] * vk[k, 8 + k + lo : 8 + k + lo + B, :]
+        return own
+
+    def before_rows(vk, w):
         prior = jnp.zeros((8, 128), F32)
         for k in range(1, CONV):
-            own = own + w[k] * vk[k, 8 + k : 8 + k + T, :]
             prior = prior + w[k] * vk[k, k : k + 8, :]
-        r.pk[j, 0 : CONV + 1, :] = jnp.concatenate(rows, axis=0)
-        return own, prior
-
+        return prior
+
+    gouts = []
     for g in range(NG):
         r.acc[1] = jnp.zeros((2, B, 128), F32)
+        take_pieces(n, me, *bwd[g])
 
         def outer(jj, carry, g=g):
             j = g * TPG + jj
             ln = lanes(j)
             e2 = spread_two(j)
-            a1 = row_state(r.ob2, j, n, 0).astype(F32)
+            a1 = row_state(laters[g], jj, n).astype(F32)
             sk = skip_row(j)
-            outs = []
-            for c in range(2):
+            ext = r.ext.at[j % 4]
+            ext[8 : 8 + T, :] = r.x[0, :, ln].astype(F32)
+            ext[0:8, :] = r.hbuf[8:16, ln].astype(F32)
+            vk = r.vk.at[j % 2]
+            w = x_weights(ln)[0]
+            rows = [jnp.zeros((1, 128), F32)] * (CONV + 1)
+            for c in (1, 0):
                 sl = blocks[c]
                 if c == 1:
                     ds = a1
                     sp = r.sb1[:, ln]
                 else:
-                    ds = keep_row(j, 1) * a1 + r.dsb1[:, ln].astype(F32)
-                    sp = row_state(r.ob, j, n, 0)
+                    ds = r.krow[1, :, ln] * a1 + r.dsb1[:, ln].astype(F32)
+                    sp = row_state(states[g], jj, n)
                 dsh = ds.astype(BF16)
                 xf = r.xc[sl, ln].astype(F32)
-                dtte = dnn(r.mt[sl, 0 : 2 * H], e2)
-                dxu = dnn(r.bcc[sl, g * 128 : (g + 1) * 128], dsh) * dtte
-                r.acc[1, c] += dnt((xf * dtte).astype(BF16), dsh)
+                dxu = dnn(r.bcc[sl, g * 128 : (g + 1) * 128], dsh) * dnn(
+                    r.mt[sl, 0 : 2 * H], e2
+                )
+                r.acc[1, c] += dnt(r.uu[sl, ln], dsh)
                 dxs = r.y[sl, ln] + dxu
                 ku = jnp.sum(xf * dxu, axis=0, keepdims=True)
-                kd = jnp.sum(ds * sp.astype(F32), axis=0, keepdims=True) * keep_row(j, c)
-                hs = head_sums(
-                    j, jnp.concatenate([xf * dxs, jnp.broadcast_to(ku + kd, (8, 128))], axis=0)
+                kd = jnp.sum(ds * sp.astype(F32), axis=0, keepdims=True) * r.krow[c, :, ln]
+                r.hsr[c : c + 1, ln] = ku + kd
+                h0, h1 = head_rows(xf * dxs)
+                r.kap[c, pl.ds(2 * j, 1), :] = h0
+                r.kap[c, pl.ds(2 * j + 1, 1), :] = h1
+                own = conv_back(
+                    c, ext, vk, w, r.cdx[sl, ln], dxs + sk * r.dy[sl, ln].astype(F32), rows
                 )
-                r.kap[:, sl] += hs[:, 0:B]
-                r.tl[:, c * 8 : (c + 1) * 8] += hs[:, B : B + 8]
-                outs.append(dxs + sk * r.dy[sl, ln].astype(F32))
-            ext = r.ext.at[j % 4]
-            ext[8 : 8 + T, :] = r.x[0, :, ln].astype(F32)
-            ext[0:8, :] = r.hbuf[8:16, ln].astype(F32)
-            own, prior = conv_back(
-                ext, r.vk.at[j % 2], x_weights(ln)[0], r.cdx[:, ln],
-                jnp.concatenate(outs, axis=0), j,
-            )
-            r.gx[:, ln] = own.astype(BF16)
-            r.tails[:, ln] = own[T - 16 : T]
-            r.hb[:, ln] = prior
+                r.gxv[g, sl, lanes(jj)] = own.astype(BF16)
+                if c == 1:
+                    r.tails[:, ln] = own[B - 16 : B]
+            r.hb[:, ln] = before_rows(vk, w)
+            r.pk[j, 0 : CONV + 1, :] = jnp.concatenate(rows, axis=0)
             give_tile(j)
             return carry
 
         lax.fori_loop(0, TPG, outer, 0, unroll=2)
+        gouts.append(
+            pltpu.make_async_copy(
+                r.gxv.at[g], r.gx.at[:, pl.ds(g * TPG * 128, TPG * 128)], r.xo.at[g]
+            )
+        )
+        gouts[-1].start()
         for c in range(2):
             r.dbc[blocks[c], g * 128 : (g + 1) * 128] += r.acc[1, c]
 
@@ -641,13 +666,19 @@
         ext = r.ext.at[j]
         ext[8 : 8 + T, :] = r.bc[:, sl].astype(F32)
         ext[0:8, :] = r.hbuf[8:16, sd].astype(F32)
-        own, prior = conv_back(
-            ext, r.vk.at[j % 2], bc_weights(j)[0], r.cdb[:, sl], r.dbc[:, sl], NT + j
-        )
+        vk = r.vk.at[j % 2]
+        w = bc_weights(j)[0]
+        rows = [jnp.zeros((1, 128), F32)] * (CONV + 1)
+        for c in (1, 0):
+            own = conv_back(
+                c, ext, vk, w, r.cdb[blocks[c], sl], r.dbc[blocks[c], sl], rows
+            )
+            r.gbc[blocks[c], sl] = own.astype(BF16)
+            if c == 1:
+                r.tails[:, sd] = own[B - 16 : B]
+        r.hb[:, sd] = before_rows(vk, w)
+        r.pk[NT + j, 0 : CONV + 1, :] = jnp.concatenate(rows, axis=0)
         r.pk[NT + j, 5:8, :] = jnp.zeros((3, 128), F32)
-        r.gbc[:, sl] = own.astype(BF16)
-        r.tails[:, sd] = own[T - 16 : T]
-        r.hb[:, sd] = prior
         give_tile(NT + j)
     back = rcopy(r.hb, r.bbuf, r.sb, r.rb_sem, {"ctx": lax.rem(me + n - 1, n)})
 
@@ -655,19 +686,23 @@
     def _():
         back.start()
 
+    of_head = (iota((H, D), 1) // HEAD_DIM == iota((H, D), 0)).astype(BF16)
+    high = r.hsr[...].astype(BF16)
+    low = (r.hsr[...] - high.astype(F32)).astype(BF16)
+    hs = dnt(of_head, high) + dnt(of_head, low)
     rev = (iota((B, B), 0) >= iota((B, B), 1)).astype(F32)
     rate_sum = jnp.zeros((H, B), F32)
     bias_sum = jnp.zeros((H, B), F32)
     for c in range(2):
         sl = blocks[c]
         dtv = r.dt[c]
-        kp = r.kap[:, sl]
-        rr = dnn_full(r.rho[:, sl] - kp, rev) + r.tl[:, c * 8 : c * 8 + 1]
+        kp = r.kap[c]
+        rr = dnn_full(r.rho[c] - kp, rev) + hs[:, c : c + 1]
         gd = (kp / dtv - rate * rr) * sigmoid(r.dtr[0, :, sl].astype(F32) + bias)
         r.gdt[:, sl] = gd
         rate_sum = rate_sum - rate * dtv * rr
         bias_sum = bias_sum + gd
-    skips = jnp.where(iota((H, B), 1) == 0, r.skc[:, 0:1], 0.0)
+    skips = jnp.where(iota((H, B), 1) == 0, hs[:, 2:3], 0.0)
     r.pk[nt - 1] = dnt_full(
         ones, jnp.concatenate([rate_sum, bias_sum, skips, jnp.zeros((H, B), F32)], axis=0)
     )
@@ -705,8 +740,12 @@
         back.wait_send()
 
     rcopy(r.kb.at[others], r.kb.at[others], r.sk, r.rk, {"ctx": me}).wait_send()
-    for sent in (r.s1, r.s2, r.s3, r.s4):
-        rcopy(r.st.at[others], r.rb.at[others], sent, sent, {"ctx": me}).wait_send()
+    for st, rb, pb, ob, s1, r1, s2, r2 in fwd + bwd:
+        rcopy(st.at[others], rb.at[others], s1, r1, {"ctx": me}).wait_send()
+        rcopy(pb.at[others], ob.at[others], s2, r2, {"ctx": me}).wait_send()
+    zout.wait()
+    for out in gouts:
+        out.wait()
 
     owns = (me < nt) & (dp == lax.rem(me, ndp))
 
@@ -725,37 +764,56 @@
     r.rh_o[...] = r.bbuf[...]
 
 
-def k5_body(scale, red, rh, tail, flg, gx_in, gbc_in,
-            gx_o, gbc_o, cw_o, cb_o, bw_o, bb_o, al_o, db_o, sk_o, ga_o):
-    f = flg[:, B:T].astype(F32)
-    lane = iota((1, B), 1)
-    last = jnp.sum(jnp.where(lane == B - 1, f, 0.0))
-    two = jnp.sum(jnp.where(lane >= B - 2, f, 0.0))
-    row = iota((16, 128), 0)
-    keep = jnp.where(row == 15, 1.0, 0.0)
-    keep = keep + jnp.where((row == 14) & (last == 0.0), 1.0, 0.0)
-    keep = keep + jnp.where((row == 13) & (two == 0.0), 1.0, 0.0)
-    for j in range(NT + 4):
-        sl = slice(j * 128, (j + 1) * 128)
-        add = jnp.concatenate([jnp.zeros((8, 128), F32), rh[:, sl]], axis=0)
-        v = (tail[:, sl] + add * keep).astype(BF16)
-        t = red[j] * scale
-        if j < NT:
-            gx_o[:, sl] = v
-            cw_o[:, sl] = t[0:4]
-            cb_o[:, sl] = t[4:5]
-            ga_o[:, sl] = t[5:6]
-        else:
-            so = slice(j * 128 - D, (j + 1) * 128 - D)
-            gbc_o[:, so] = v
-            i, sb = (j - NT) // 2, slice(((j - NT) % 2) * 128, ((j - NT) % 2) * 128 + 128)
-            for k in range(CONV):
-                bw_o[k, i : i + 1, sb] = t[k : k + 1]
-            bb_o[i : i + 1, sb] = t[4:5]
-    last_tile = red[NT + 4] * scale
-    al_o[...] = last_tile[0:1, 0:H]
-    db_o[...] = last_tile[0:1, H : 2 * H]
-    sk_o[...] = last_tile[0:1, 2 * H : 3 * H]
+def k5_body(scale, red, rh, tail, flg, gx_i, dz_i, gbc_i, gdt_i,
+            gx_o, dz_o, gbc_o, gdt_o, cw_o, cb_o, bw_o, bb_o, al_o, db_o, sk_o, ga_o, gbs):
+    i = pl.program_id(0)
+    last_step = pl.num_programs(0) - 1
+    rows = gx_o.shape[0]
+    gx_o[...] = gx_i[...]
+    dz_o[...] = dz_i[...]
+    gbs[...] = gbc_i[...]
+
+    @pl.when(i == 0)
+    def _():
+        gdt_o[...] = gdt_i[...]
+        for j in range(NT + 4):
+            sl = slice(j * 128, (j + 1) * 128)
+            t = red[j] * scale
+            if j < NT:
+                cw_o[:, sl] = t[0:4]
+                cb_o[:, sl] = t[4:5]
+                ga_o[:, sl] = t[5:6]
+            else:
+                m = j - NT
+                sb = slice((m % 2) * 128, (m % 2) * 128 + 128)
+                for k in range(CONV):
+                    bw_o[k, m // 2 : m // 2 + 1, sb] = t[k : k + 1]
+                bb_o[m // 2 : m // 2 + 1, sb] = t[4:5]
+        last_tile = red[NT + 4] * scale
+        al_o[...] = last_tile[0:1, 0:H]
+        db_o[...] = last_tile[0:1, H : 2 * H]
+        sk_o[...] = last_tile[0:1, 2 * H : 3 * H]
+
+    @pl.when(i == last_step)
+    def _():
+        f = flg[:, B:T].astype(F32)
+        lane = iota((1, B), 1)
+        last = jnp.sum(jnp.where(lane == B - 1, f, 0.0))
+        two = jnp.sum(jnp.where(lane >= B - 2, f, 0.0))
+        row = iota((16, 128), 0)
+        keep = jnp.where(row == 15, 1.0, 0.0)
+        keep = keep + jnp.where((row == 14) & (last == 0.0), 1.0, 0.0)
+        keep = keep + jnp.where((row == 13) & (two == 0.0), 1.0, 0.0)
+        for j in range(NT + 4):
+            sl = slice(j * 128, (j + 1) * 128)
+            add = jnp.concatenate([jnp.zeros((8, 128), F32), rh[:, sl]], axis=0)
+            v = (tail[:, sl] + add * keep).astype(BF16)
+            if j < NT:
+                gx_o[rows - 16 : rows, sl] = v
+            else:
+                gbs[rows - 16 : rows, j * 128 - D : (j + 1) * 128 - D] = v
+
+    gbc_o[...] = gbs[...].reshape(rows, 2, DB // 2)
 
 
 def sds(*shape, dtype=F32):
@@ -775,7 +833,7 @@
     ne = n * ndp
     ANY = pl.BlockSpec(memory_space=pl.ANY)
     ins = [
-        ("x", x_raw, VM), ("bc", bc_raw[0].reshape(T, DB), VM), ("z_hbm", z_gate, ANY),
+        ("x", x_raw, VM), ("bc_raw", bc_raw, VM), ("z_hbm", z_gate, ANY),
         ("go_hbm", grad_out, ANY), ("dtr", dt_raw, VM), ("flg", resets, VM),
         ("alog", a_log.reshape(1, H), VM), ("dtb", dt_bias.reshape(1, H), VM),
         ("cxw", conv_x_weight, VM), ("cxb", conv_x_bias.reshape(1, D), VM),
@@ -783,13 +841,13 @@
         ("gain", norm_gain.reshape(1, D), VM), ("skip", skip_weight, SM),
     ]
     outs = [
-        ("gx", sds(T, D, dtype=BF16)), ("gbc", sds(T, DB, dtype=BF16)),
-        ("dz", sds(T, D, dtype=BF16)), ("gdt", sds(H, T)), ("tails", sds(16, D + DB)),
+        ("gx", sds(T, D, dtype=BF16)), ("dz", sds(T, D, dtype=BF16)),
+        ("gbc", sds(T, DB, dtype=BF16)), ("gdt", sds(H, T)), ("tails", sds(16, D + DB)),
         ("red", sds(nt, 8, 128)), ("rh_o", sds(8, D + DB)),
     ]
     V = pltpu.VMEM
     dma = pltpu.SemaphoreType.DMA
-    state = V((n, ROWS, w), BF16)
+    state = V((n, ROWS, w // NG), BF16)
     scratch = [
         ("z", V((T, D), BF16)), ("go", V((T, D), BF16)), ("zs", dma), ("gs", dma),
         ("ext", V((4, T + 8, 128), F32)), ("cnt", V((T + 8, 128), F32)),
@@ -798,35 +856,39 @@
         ("rs", V((T, 128), BF16)), ("tail", V((16, D + DB), BF16)),
         ("hbuf", V((16, D + DB), BF16)), ("xc", V((T, D), BF16)), ("bcc", V((T, DB), BF16)),
         ("cdb", V((T, DB), F32)), ("cdx", V((T, D), F32)), ("fr", V((2, NSTATE, D), F32)),
-        ("kr", V((ncq, 1, w), F32)), ("kb", V((n, 1, w), F32)), ("gm", V((B, B), F32)),
+        ("kr", V((ncq, 1, w), F32)), ("kb", V((n, 1, w), F32)), ("krow", V((2, 1, D), F32)),
+        ("uu", V((T, D), BF16)), ("bc", V((T, DB), BF16)), ("hsr", V((8, D), F32)),
+        ("dzv", V((T, D), BF16)), ("gxv", V((NG, T, D // NG), BF16)), ("zo", dma),
+        ("xo", dma((NG,))), ("gm", V((B, B), F32)),
         ("lm", V((2 * NT, 2 * B, B), F32)), ("wm", V((2 * NT, 2 * B, B), BF16)),
         ("y", V((T, D), F32)), ("gate", V((T, D), F32)), ("dgate", V((T, D), F32)),
         ("mixed", V((T, D), BF16)), ("sb1", V((NSTATE, D), BF16)),
         ("sums_acc", V((2, T, 128), F32)), ("sums", V((16, T), F32)),
         ("sbuf", V((nh, 16, T), F32)), ("inv", V((T, 128), F32)), ("coef", V((T, 128), F32)),
-        ("rho", V((H, T), F32)), ("skc", V((H, 8), F32)), ("dy", V((T, D), BF16)),
+        ("rho", V((2, H, B), F32)), ("dy", V((T, D), BF16)),
         ("fd", V((T, D), BF16)), ("dsb1", V((NSTATE, D), BF16)), ("acc", V((2, 2, B, 128), F32)),
-        ("dbc", V((T, DB), F32)), ("kap", V((H, T), F32)), ("tl", V((H, 16), F32)),
+        ("dbc", V((T, DB), F32)), ("kap", V((2, H, B), F32)),
         ("vk", V((2, CONV, T + 16, 128), F32)), ("pk", V((nt, 8, 128), F32)),
         ("prb", V((ne, 8, 128), F32)), ("pob", V((nt, 8, 128), F32)),
         ("hb", V((8, D + DB), F32)), ("bbuf", V((8, D + DB), F32)),
-        ("st", state), ("rb", state), ("pb", state), ("ob", state),
-        ("ad", state), ("rb2", state), ("pb2", state), ("ob2", state),
         ("sh", dma), ("rh", dma), ("sb", dma), ("rb_sem", dma),
         ("hs", dma((nh,))), ("hr", dma((nh,))),
     ]
     scratch += [
         (k, dma)
         for k in (
-            "s1", "r1", "s2", "r2", "s3", "r3", "s4", "r4", "sk", "rk", "ps", "ar", "pr", "as_"
+            "sk", "rk", "ps", "ar", "pr", "as_",
         )
     ]
+    for way in ("f0", "f1", "b0", "b1"):
+        scratch += [(k + way, state) for k in ("st", "rb", "pb", "ob")]
+        scratch += [(k + way, dma) for k in ("s1", "r1", "s2", "r2")]
     names = [v[0] for v in ins] + [v[0] for v in outs] + [v[0] for v in scratch]
-    gx, gbc, dz, gdt, tails, red, rh = pl.pallas_call(
+    gx, dz, gbc, gdt, tails, red, rh = pl.pallas_call(
         functools.partial(main_body, n, nh, ndp, nt, names),
         out_shape=[v[1] for v in outs],
         in_specs=[v[2] for v in ins],
-        out_specs=[VM] * len(outs),
+        out_specs=[ANY] * 2 + [VM] * (len(outs) - 2),
         scratch_shapes=[v[1] for v in scratch],
         compiler_params=pltpu.CompilerParams(
             vmem_limit_bytes=VLIM, collective_id=0, has_side_effects=True
@@ -834,28 +896,30 @@
     )(*[v[1] for v in ins])
     scale = float(ndp * n * T) ** (-0.5)
     whole = lambda *s: pl.BlockSpec(s, lambda i: (0,) * len(s))
+    step = T // 4
+    block = lambda c: pl.BlockSpec((step, c), lambda i: (i, 0))
     outs = pl.pallas_call(
         functools.partial(k5_body, scale),
-        grid=(1,),
+        grid=(4,),
         out_shape=(
-            sds(T, D, dtype=BF16), sds(T, DB, dtype=BF16), sds(CONV, D), sds(1, D),
-            sds(CONV, 2, DB // 2), sds(2, DB // 2), sds(1, H), sds(1, H), sds(1, H), sds(1, D),
+            sds(T, D, dtype=BF16), sds(T, D, dtype=BF16), sds(T, 2, DB // 2, dtype=BF16),
+            sds(H, T), sds(CONV, D), sds(1, D), sds(CONV, 2, DB // 2), sds(2, DB // 2),
+            sds(1, H), sds(1, H), sds(1, H), sds(1, D),
         ),
         in_specs=[
             whole(nt, 8, 128), whole(8, D + DB), whole(16, D + DB), whole(1, T),
-            pl.BlockSpec(memory_space=pl.ANY), pl.BlockSpec(memory_space=pl.ANY),
+            block(D), block(D), block(DB), whole(H, T),
         ],
         out_specs=[
-            pl.BlockSpec((16, D), lambda i: (T // 16 - 1, 0)),
-            pl.BlockSpec((16, DB), lambda i: (T // 16 - 1, 0)),
-            whole(CONV, D), whole(1, D), whole(CONV, 2, DB // 2), whole(2, DB // 2),
+            block(D), block(D), pl.BlockSpec((step, 2, DB // 2), lambda i: (i, 0, 0)),
+            whole(H, T), whole(CONV, D), whole(1, D), whole(CONV, 2, DB // 2), whole(2, DB // 2),
             whole(1, H), whole(1, H), whole(1, H), whole(1, D),
         ],
-        input_output_aliases={4: 0, 5: 1},
-    )(red, rh, tails, resets, gx, gbc)
-    gx, gbc, cw, cb, bw, bb, al, db, sk, ga = outs
+        scratch_shapes=[V((step, DB), BF16)],
+    )(red, rh, tails, resets, gx, dz, gbc, gdt)
+    gx, dz, gbc, gdt, cw, cb, bw, bb, al, db, sk, ga = outs
     return (
-        gx[None], gbc.reshape(1, T, 2, DB // 2), dz[None], gdt[None], cw, cb.reshape(D),
+        gx[None], gbc[None], dz[None], gdt[None], cw, cb.reshape(D),
         bw, bb, al.reshape(H), db.reshape(H), sk.reshape(H), ga.reshape(D),
     )
 

time: 126 us -> 99.9 us (0.79)
  Pallas kernels: 118 us -> 99.1 us
  local copies, waits for them, and re-layouts: 7.39 us -> 0 us
    pallas_call x1, Pallas kernels: 116 us -> 94.8 us  [per_device(): pl.pallas_call(functools.partial(main_body, n, nh, ndp, nt, names), out_s...]
    unnamed x8 -> x0, local copies, waits for them, and re-layouts: 5.67 us -> none
    pallas_call x1, Pallas kernels: 1.79 us -> 4.33 us  [per_device(): pl.pallas_call(functools.partial(k5_body, scale), grid=(4,), out_shape=(s...]
    reshape x1 -> x0, local copies, waits for them, and re-layouts: 1.72 us -> none  [per_device(): gbc.reshape(1, T, 2, DB // 2)]
where the time goes in v4:
time: 99.9 us; the launch traced here: 99.7 us
  Pallas kernels  99.1 us (99%)
    pallas_call x1, Pallas kernels, per_device(): pl.pallas_call(functools.partial(main_body, n, nh, ndp, nt, names), out_s...  94.8 us
    pallas_call x1, Pallas kernels, per_device(): pl.pallas_call(functools.partial(k5_body, scale), grid=(4,), out_shape=(s...  4.33 us

profile of v4, /device:TPU:1, one launch (start us, length us, event | category | flops | bytes accessed | tf_op | source)
XLA Modules:
  0.0 99.7 jit_solution(12743976927339954522)
XLA Ops:
  0.6 94.8 %shard_map.229 = (bf16[256,2048]{1,0:T(8,128)(2,1)}, bf16[256,2048]{1,0:T(8,128)(2,1)}, bf16[256,512]{1,0:T(8,128)(2,1)}, f32[32,256]{1,0:T(8,128)}, f32[16,2560...) custom-call(bf16[1,256,2048]{2,1,0:T(8,128)(2,1)} %refs_0_.1, bf16[1,256,2,256]{3,2,1,0:T(2,128)(2,1)} %refs_1_.1, ...), custom_call_target="tpu_custom_call" | custom-call | tf_op jit(solution)/shard_map/pallas_call | solution.py:887
  95.4 4.3 %shard_map.230 = (bf16[256,2048]{1,0:T(8,128)(2,1)}, bf16[256,2048]{1,0:T(8,128)(2,1)}, bf16[256,2,256]{2,1,0:T(2,128)(2,1)}, f32[32,256]{1,0:T(8,128)}, f32[4,2...) custom-call(f32[21,8,128]{2,1,0:T(8,128)} %get-tuple-element.31.red,, ...), custom_call_target="tpu_custom_call" | custom-call | tf_op jit(solution)/shard_map/pallas_call | solution.py:901

commit v5 on v4

--- a/solution.py
+++ b/solution.py
@@ -31,7 +31,7 @@
 ROWS = 16
 VM = pl.BlockSpec(memory_space=pltpu.VMEM)
 SM = pl.BlockSpec(memory_space=pltpu.SMEM)
-VLIM = 60 * 1024 * 1024
+VMAIN = 46 * 1024 * 1024
 
 
 def dnn(a, b):
@@ -184,7 +184,7 @@
     rcopy(pb.at[others], ob.at[others], s2, r2, {"ctx": me}).wait_recv()
 
 
-def main_body(n, nh, ndp, nt, names, *refs):
+def main_body(n, nh, ndp, nt, names, fed, *refs):
     r = types.SimpleNamespace(**dict(zip(names, refs)))
     ncq = n // 8
     wh = TPG * 128 // ncq
@@ -219,12 +219,20 @@
         pl.semaphore_signal(
             barrier, inc=1, device_id={"head": lax.rem(hd + k, nh)}, device_id_type=MESH
         )
+    loads = [
+        pltpu.make_async_copy(getattr(r, k + "_in"), getattr(r, k), r.ins.at[i])
+        for i, k in enumerate(fed)
+    ]
+    for load in loads:
+        load.start()
     zcopy = pltpu.make_async_copy(r.z_hbm.at[0], r.z, r.zs)
     gcopy = pltpu.make_async_copy(r.go_hbm.at[0], r.go, r.gs)
     zcopy.start()
     gcopy.start()
+    r.hsr[...] = jnp.zeros_like(r.hsr)
+    for load in loads:
+        load.wait()
     r.bc[...] = r.bc_raw[0].reshape(T, DB)
-    r.hsr[...] = jnp.zeros_like(r.hsr)
 
     rate = jnp.exp(column(r.alog[...]))
     bias = column(r.dtb[...])
@@ -508,7 +516,7 @@
                     gi = r.go[sl, ln].astype(F32) * r.inv[sl, :]
                     dg = gi * r.gain[0:1, ln] - gated * r.coef[sl, :]
                     grow = grow + jnp.sum(gi * gated, axis=0, keepdims=True)
-                    r.dzv[sl, ln] = (dg * m * r.dgate[sl, ln]).astype(BF16)
+                    r.dz[sl, ln] = (dg * m * r.dgate[sl, ln]).astype(BF16)
                     dm = (dg * gt).astype(BF16)
                     r.dy[sl, ln] = dm
                     dy = dm.astype(F32)
@@ -532,9 +540,6 @@
             lax.fori_loop(0, 4, gates, 0, unroll=4)
             for cq in range(hf * ncq // 2, (hf + 1) * ncq // 2):
                 send_pieces(n, cq, me, *bwd[g])
-    zout = pltpu.make_async_copy(r.dzv, r.dz, r.zo)
-    zout.start()
-
     for g in range(NG):
         r.acc[...] = jnp.zeros_like(r.acc)
 
@@ -601,7 +606,6 @@
             prior = prior + w[k] * vk[k, k : k + 8, :]
         return prior
 
-    gouts = []
     for g in range(NG):
         r.acc[1] = jnp.zeros((2, B, 128), F32)
         take_pieces(n, me, *bwd[g])
@@ -642,7 +646,7 @@
                 own = conv_back(
                     c, ext, vk, w, r.cdx[sl, ln], dxs + sk * r.dy[sl, ln].astype(F32), rows
                 )
-                r.gxv[g, sl, lanes(jj)] = own.astype(BF16)
+                r.gx[sl, ln] = own.astype(BF16)
                 if c == 1:
                     r.tails[:, ln] = own[B - 16 : B]
             r.hb[:, ln] = before_rows(vk, w)
@@ -651,12 +655,6 @@
             return carry
 
         lax.fori_loop(0, TPG, outer, 0, unroll=2)
-        gouts.append(
-            pltpu.make_async_copy(
-                r.gxv.at[g], r.gx.at[:, pl.ds(g * TPG * 128, TPG * 128)], r.xo.at[g]
-            )
-        )
-        gouts[-1].start()
         for c in range(2):
             r.dbc[blocks[c], g * 128 : (g + 1) * 128] += r.acc[1, c]
 
@@ -743,9 +741,6 @@
     for st, rb, pb, ob, s1, r1, s2, r2 in fwd + bwd:
         rcopy(st.at[others], rb.at[others], s1, r1, {"ctx": me}).wait_send()
         rcopy(pb.at[others], ob.at[others], s2, r2, {"ctx": me}).wait_send()
-    zout.wait()
-    for out in gouts:
-        out.wait()
 
     owns = (me < nt) & (dp == lax.rem(me, ndp))
 
@@ -761,59 +756,49 @@
         rcopy(r.pk, r.pob, r.ps, r.ar, {"ctx": me}).wait()
 
     r.red[...] = r.pob[...]
-    r.rh_o[...] = r.bbuf[...]
-
-
-def k5_body(scale, red, rh, tail, flg, gx_i, dz_i, gbc_i, gdt_i,
-            gx_o, dz_o, gbc_o, gdt_o, cw_o, cb_o, bw_o, bb_o, al_o, db_o, sk_o, ga_o, gbs):
-    i = pl.program_id(0)
-    last_step = pl.num_programs(0) - 1
-    rows = gx_o.shape[0]
-    gx_o[...] = gx_i[...]
-    dz_o[...] = dz_i[...]
+    alike = r.cnt[T : T + 8, :] == r.cnt[T + 7 : T + 8, :]
+    for j in range(NT + 4):
+        sl = slice(j * 128, (j + 1) * 128)
+        r.rh_o[:, sl] = jnp.where(alike, r.bbuf[:, sl], 0.0)
+
+
+def k5_body(scale, red, rh, tail, gx_i, dz_i, gbc_i, gdt_i,
+            gx_o, dz_o, gbc_o, gdt_o, cw_o, cb_o, bw_o, bb_o, al_o, db_o, sk_o, ga_o,
+            gxt, gbs, sems):
+    copies = [
+        pltpu.make_async_copy(gx_i.at[0 : T - 16], gx_o.at[0 : T - 16], sems.at[0]),
+        pltpu.make_async_copy(dz_i, dz_o, sems.at[1]),
+    ]
+    for cp in copies:
+        cp.start()
+    gdt_o[...] = gdt_i[...]
     gbs[...] = gbc_i[...]
-
-    @pl.when(i == 0)
-    def _():
-        gdt_o[...] = gdt_i[...]
-        for j in range(NT + 4):
-            sl = slice(j * 128, (j + 1) * 128)
-            t = red[j] * scale
-            if j < NT:
-                cw_o[:, sl] = t[0:4]
-                cb_o[:, sl] = t[4:5]
-                ga_o[:, sl] = t[5:6]
-            else:
-                m = j - NT
-                sb = slice((m % 2) * 128, (m % 2) * 128 + 128)
-                for k in range(CONV):
-                    bw_o[k, m // 2 : m // 2 + 1, sb] = t[k : k + 1]
-                bb_o[m // 2 : m // 2 + 1, sb] = t[4:5]
-        last_tile = red[NT + 4] * scale
-        al_o[...] = last_tile[0:1, 0:H]
-        db_o[...] = last_tile[0:1, H : 2 * H]
-        sk_o[...] = last_tile[0:1, 2 * H : 3 * H]
-
-    @pl.when(i == last_step)
-    def _():
-        f = flg[:, B:T].astype(F32)
-        lane = iota((1, B), 1)
-        last = jnp.sum(jnp.where(lane == B - 1, f, 0.0))
-        two = jnp.sum(jnp.where(lane >= B - 2, f, 0.0))
-        row = iota((16, 128), 0)
-        keep = jnp.where(row == 15, 1.0, 0.0)
-        keep = keep + jnp.where((row == 14) & (last == 0.0), 1.0, 0.0)
-        keep = keep + jnp.where((row == 13) & (two == 0.0), 1.0, 0.0)
-        for j in range(NT + 4):
-            sl = slice(j * 128, (j + 1) * 128)
-            add = jnp.concatenate([jnp.zeros((8, 128), F32), rh[:, sl]], axis=0)
-            v = (tail[:, sl] + add * keep).astype(BF16)
-            if j < NT:
-                gx_o[rows - 16 : rows, sl] = v
-            else:
-                gbs[rows - 16 : rows, j * 128 - D : (j + 1) * 128 - D] = v
-
-    gbc_o[...] = gbs[...].reshape(rows, 2, DB // 2)
+    for j in range(NT + 4):
+        sl = slice(j * 128, (j + 1) * 128)
+        add = jnp.concatenate([jnp.zeros((8, 128), F32), rh[:, sl]], axis=0)
+        v = (tail[:, sl] + add).astype(BF16)
+        t = red[j] * scale
+        if j < NT:
+            gxt[:, sl] = v
+            cw_o[:, sl] = t[0:4]
+            cb_o[:, sl] = t[4:5]
+            ga_o[:, sl] = t[5:6]
+        else:
+            m = j - NT
+            gbs[T - 16 : T, m * 128 : (m + 1) * 128] = v
+            sb = slice((m % 2) * 128, (m % 2) * 128 + 128)
+            for k in range(CONV):
+                bw_o[k, m // 2 : m // 2 + 1, sb] = t[k : k + 1]
+            bb_o[m // 2 : m // 2 + 1, sb] = t[4:5]
+    copies.append(pltpu.make_async_copy(gxt, gx_o.at[T - 16 : T], sems.at[2]))
+    copies[-1].start()
+    gbc_o[...] = gbs[...].reshape(T, 2, DB // 2)
+    last_tile = red[NT + 4] * scale
+    al_o[...] = last_tile[0:1, 0:H]
+    db_o[...] = last_tile[0:1, H : 2 * H]
+    sk_o[...] = last_tile[0:1, 2 * H : 3 * H]
+    for cp in copies:
+        cp.wait()
 
 
 def sds(*shape, dtype=F32):
@@ -831,15 +816,17 @@
     w = D // ncq
     nt = NT + 5
     ne = n * ndp
-    ANY = pl.BlockSpec(memory_space=pl.ANY)
-    ins = [
-        ("x", x_raw, VM), ("bc_raw", bc_raw, VM), ("z_hbm", z_gate, ANY),
-        ("go_hbm", grad_out, ANY), ("dtr", dt_raw, VM), ("flg", resets, VM),
-        ("alog", a_log.reshape(1, H), VM), ("dtb", dt_bias.reshape(1, H), VM),
-        ("cxw", conv_x_weight, VM), ("cxb", conv_x_bias.reshape(1, D), VM),
-        ("cbw", conv_bc_weight, VM), ("cbb", conv_bc_bias, VM),
-        ("gain", norm_gain.reshape(1, D), VM), ("skip", skip_weight, SM),
+    HB = pl.BlockSpec(memory_space=pltpu.HBM)
+    taken = [
+        ("x", x_raw), ("bc_raw", bc_raw), ("dtr", dt_raw), ("flg", resets),
+        ("alog", a_log.reshape(1, H)), ("dtb", dt_bias.reshape(1, H)), ("cxw", conv_x_weight),
+        ("cxb", conv_x_bias.reshape(1, D)), ("cbw", conv_bc_weight), ("cbb", conv_bc_bias),
+        ("gain", norm_gain.reshape(1, D)), ("skip", skip_weight),
     ]
+    fed = [k for k, v in taken]
+    held = lambda v: pltpu.with_memory_space_constraint(v, pltpu.HBM)
+    ins = [(k + "_in", held(v), HB) for k, v in taken]
+    ins += [("z_hbm", held(z_gate), HB), ("go_hbm", held(grad_out), HB)]
     outs = [
         ("gx", sds(T, D, dtype=BF16)), ("dz", sds(T, D, dtype=BF16)),
         ("gbc", sds(T, DB, dtype=BF16)), ("gdt", sds(H, T)), ("tails", sds(16, D + DB)),
@@ -858,8 +845,7 @@
         ("cdb", V((T, DB), F32)), ("cdx", V((T, D), F32)), ("fr", V((2, NSTATE, D), F32)),
         ("kr", V((ncq, 1, w), F32)), ("kb", V((n, 1, w), F32)), ("krow", V((2, 1, D), F32)),
         ("uu", V((T, D), BF16)), ("bc", V((T, DB), BF16)), ("hsr", V((8, D), F32)),
-        ("dzv", V((T, D), BF16)), ("gxv", V((NG, T, D // NG), BF16)), ("zo", dma),
-        ("xo", dma((NG,))), ("gm", V((B, B), F32)),
+ ("gm", V((B, B), F32)),
         ("lm", V((2 * NT, 2 * B, B), F32)), ("wm", V((2 * NT, 2 * B, B), BF16)),
         ("y", V((T, D), F32)), ("gate", V((T, D), F32)), ("dgate", V((T, D), F32)),
         ("mixed", V((T, D), BF16)), ("sb1", V((NSTATE, D), BF16)),
@@ -880,43 +866,36 @@
             "sk", "rk", "ps", "ar", "pr", "as_",
         )
     ]
+    scratch += [
+        (k, (pltpu.SMEM if k == "skip" else V)(v.shape, v.dtype)) for k, v in taken
+    ] + [("ins", dma((len(taken),)))]
     for way in ("f0", "f1", "b0", "b1"):
         scratch += [(k + way, state) for k in ("st", "rb", "pb", "ob")]
         scratch += [(k + way, dma) for k in ("s1", "r1", "s2", "r2")]
     names = [v[0] for v in ins] + [v[0] for v in outs] + [v[0] for v in scratch]
     gx, dz, gbc, gdt, tails, red, rh = pl.pallas_call(
-        functools.partial(main_body, n, nh, ndp, nt, names),
+        functools.partial(main_body, n, nh, ndp, nt, names, fed),
         out_shape=[v[1] for v in outs],
         in_specs=[v[2] for v in ins],
-        out_specs=[ANY] * 2 + [VM] * (len(outs) - 2),
+        out_specs=[VM] * len(outs),
         scratch_shapes=[v[1] for v in scratch],
         compiler_params=pltpu.CompilerParams(
-            vmem_limit_bytes=VLIM, collective_id=0, has_side_effects=True
+            vmem_limit_bytes=VMAIN, collective_id=0, has_side_effects=True
         ),
     )(*[v[1] for v in ins])
     scale = float(ndp * n * T) ** (-0.5)
-    whole = lambda *s: pl.BlockSpec(s, lambda i: (0,) * len(s))
-    step = T // 4
-    block = lambda c: pl.BlockSpec((step, c), lambda i: (i, 0))
     outs = pl.pallas_call(
         functools.partial(k5_body, scale),
-        grid=(4,),
         out_shape=(
             sds(T, D, dtype=BF16), sds(T, D, dtype=BF16), sds(T, 2, DB // 2, dtype=BF16),
             sds(H, T), sds(CONV, D), sds(1, D), sds(CONV, 2, DB // 2), sds(2, DB // 2),
             sds(1, H), sds(1, H), sds(1, H), sds(1, D),
         ),
-        in_specs=[
-            whole(nt, 8, 128), whole(8, D + DB), whole(16, D + DB), whole(1, T),
-            block(D), block(D), block(DB), whole(H, T),
-        ],
-        out_specs=[
-            block(D), block(D), pl.BlockSpec((step, 2, DB // 2), lambda i: (i, 0, 0)),
-            whole(H, T), whole(CONV, D), whole(1, D), whole(CONV, 2, DB // 2), whole(2, DB // 2),
-            whole(1, H), whole(1, H), whole(1, H), whole(1, D),
-        ],
-        scratch_shapes=[V((step, DB), BF16)],
-    )(red, rh, tails, resets, gx, dz, gbc, gdt)
+        in_specs=[VM] * 7,
+        out_specs=[HB, HB] + [VM] * 10,
+        scratch_shapes=[V((16, D), BF16), V((T, DB), BF16), dma((3,))],
+        compiler_params=pltpu.CompilerParams(vmem_limit_bytes=16 * 1024 * 1024),
+    )(red, rh, tails, gx, dz, gbc, gdt)
     gx, dz, gbc, gdt, cw, cb, bw, bb, al, db, sk, ga = outs
     return (
         gx[None], gbc[None], dz[None], gdt[None], cw, cb.reshape(D),

time: 99.9 us -> 96 us (0.961)
  Pallas kernels: 99.1 us -> 95.3 us
    pallas_call x2, Pallas kernels: 99.1 us -> 95.3 us  [the longest x1 93.2 us: per_device(): pl.pallas_call(functools.partial(main_body, n, nh, ndp, nt, names, fed),...]
where the time goes in v5:
time: 96 us; the launch traced here: 95.9 us
  Pallas kernels  95.3 us (99%)
    pallas_call x1, Pallas kernels, per_device(): pl.pallas_call(functools.partial(main_body, n, nh, ndp, nt, names, fed),...  93.2 us
    pallas_call x1, Pallas kernels, per_device(): pl.pallas_call(functools.partial(k5_body, scale), out_shape=(sds(T, D, dt...  2.07 us

profile of v5, /device:TPU:1, one launch (start us, length us, event | category | flops | bytes accessed | tf_op | source)
XLA Modules:
  0.0 95.9 jit_solution(2736528390237880529)
XLA Ops:
  0.6 93.2 %shard_map.229 = (bf16[256,2048]{1,0:T(8,128)(2,1)S(1)}, bf16[256,2048]{1,0:T(8,128)(2,1)S(1)}, bf16[256,512]{1,0:T(8,128)(2,1)S(1)}, f32[32,256]{1,0:T(8,128)S(...) custom-call(bf16[1,256,2048]{2,1,0:T(8,128)(2,1)} %refs_0_.1, ...), custom_call_target="tpu_custom_call" | custom-call | tf_op jit(solution)/shard_map/pallas_call | solution.py:876
  93.9 2.1 %shard_map.230 = (bf16[256,2048]{1,0:T(8,128)(2,1)}, bf16[256,2048]{1,0:T(8,128)(2,1)}, bf16[256,2,256]{2,1,0:T(2,128)(2,1)}, f32[32,256]{1,0:T(8,128)}, f32[4,2...) custom-call(f32[21,8,128]{2,1,0:T(8,128)S(1)} %get-tuple-element.31., ...), custom_call_target="tpu_custom_call" | custom-call | tf_op jit(solution)/shard_map/pallas_call | solution.py:887
